TPU v7x, 512 devices: a whole 4x8x8 slice. The times are simulated.
512 devices in a mesh: stream: 128 (over y, z, core), vert: 4 (over x).
Axes of the slice: x: 4, y: 8, z: 8, core: 2. Of those that a mesh axis runs over, the one named last changes fastest.
Arguments:
- particles: float32 [4096, 4, 7, 128], P('stream', 'vert'), may hold values from -4 to 4, as said below
- phase_flags: int32 [4096, 4, 128], P('stream', 'vert'), may hold values 0 or 1
- neighbours: int32 [4096, 4, 4], P('stream', 'vert'), may hold values from 0 to 7, as said below
- history: bfloat16 [4096, 4, 3, 126, 128], P('stream', 'vert'), may hold values from -160 to 160
- basis_start: float32 [128, 64], replicated, may hold values from -0.5 to 0.5
Outputs:
- new_state: float32 [4096, 4, 7, 128], P('stream', 'vert')
- filtered: float32 [4096, 4, 3, 128], P('stream', 'vert')
Inputs may be any that keep to these rules, and one draw needn't show every extreme that they name: `particles`: rows 0 to 2 of a particle lie in 0 to 2, rows 3 to 5 in -4 to 4, row 6 in 0.97 to 1.03. `neighbours`: the 4 codes of one block are distinct.
All inputs are finite; a program needn't handle non-finite values. No bound on the sum of `phase_flags` on one device may be relied on, other than what follows from the above.
Results may differ from a plain program's by a relative error of at most 0.0003.
Values sent between devices are 32-bit elements; how exact they have to be, the bound alone decides.
A program may use at most 64 MiB of HBM per device.

v0:
```python
import math

import jax
import jax.numpy as jnp
from jax import lax
from jax.sharding import PartitionSpec as P

POD_ITERS = 4


ALPHA_KERNEL = 21.0 / (16.0 * math.pi)
VOLUME = 1.0 / 16.0
STIFFNESS = 100.0 / 7.0
TIME_STEP = 0.02
GRAVITY = 1.0
SEDIMENT_EXTRA = 1.65


def with_halo(block, sides, width):
    for axis, dim in sides:
        count = lax.axis_size(axis)
        forward = [(i, i + 1) for i in range(count - 1)]
        backward = [(target, source) for source, target in forward]
        low = lax.ppermute(
            lax.slice_in_dim(block, block.shape[dim] - width, None, axis=dim), axis, forward
        )
        high = lax.ppermute(lax.slice_in_dim(block, 0, width, axis=dim), axis, backward)
        block = jnp.concatenate([low, block, high], axis=dim)
    return block


def forces(own_block, near_blocks, cell_shifts):
    separation = (
        own_block[:, None, 0:3, :, None]
        - near_blocks[:, :, 0:3, None, :]
        - cell_shifts[:, :, :, None, None]
    )
    radius = jnp.sqrt(jnp.sum(separation * separation, axis=2))
    kernel_reach = jnp.maximum(1.0 - 0.5 * radius, 0.0)
    kernel_slope = -5.0 * ALPHA_KERNEL * kernel_reach**3 * near_blocks[:, :, 6, None, :]
    closing = own_block[:, None, 3:6, :, None] - near_blocks[:, :, 3:6, None, :]
    density_rate = jnp.sum(kernel_slope * jnp.sum(closing * separation, axis=2), axis=(1, 3))
    pressure_term = kernel_slope * (own_block[:, None, 7, :, None] + near_blocks[:, :, 7, None, :])
    acceleration = -jnp.sum(pressure_term[:, :, None] * separation, axis=(1, 4))
    return (acceleration, density_rate)


def block_layout(neighbours):
    blocks_stream, blocks_vert = (neighbours.shape[0], neighbours.shape[1])
    offset_code = neighbours + (neighbours >= 4).astype(jnp.int32)
    zero_codes = jnp.zeros((blocks_stream, blocks_vert, 1), jnp.int32)
    stream_step = jnp.concatenate([zero_codes, offset_code // 3 - 1], axis=-1)
    vert_step = jnp.concatenate([zero_codes, offset_code % 3 - 1], axis=-1)
    stream_place = jnp.arange(blocks_stream, dtype=jnp.int32)[:, None, None]
    vert_place = jnp.arange(blocks_vert, dtype=jnp.int32)[None, :, None]
    near_index = (stream_place + 1 + stream_step) * (blocks_vert + 2) + (vert_place + 1 + vert_step)
    list_width = near_index.shape[2]
    cell_shifts = jnp.stack(
        [
            2.0 * stream_step.astype(jnp.float32),
            jnp.zeros(stream_step.shape, jnp.float32),
            2.0 * vert_step.astype(jnp.float32),
        ],
        axis=-1,
    )
    return (near_index.reshape(-1, list_width), cell_shifts.reshape(-1, list_width, 3))


def make_payload(particles, rest_density, particle_mass):
    relative = particles[:, :, 6]
    pressure = STIFFNESS * (relative**7 - 1.0) / (rest_density * relative * relative)
    return jnp.concatenate(
        [particles[:, :, 0:6], particle_mass[:, :, None], pressure[:, :, None]], axis=2
    )


def interact(payload, extended, near_index, cell_shifts, group_limit):
    block_count = payload.shape[0] * payload.shape[1]
    group_size = math.gcd(block_count, group_limit)
    flat_blocks = extended.reshape(-1, 8, payload.shape[3])
    list_width = near_index.shape[1]

    def one_group(pieces):
        own_block, index_part, shift_part = pieces
        near_blocks = jnp.take(flat_blocks, index_part, axis=0)
        return forces(own_block, near_blocks, shift_part)

    acceleration, density_rate = lax.map(
        one_group,
        (
            payload.reshape(block_count // group_size, group_size, 8, -1),
            near_index.reshape(-1, group_size, list_width),
            cell_shifts.reshape(-1, group_size, list_width, 3),
        ),
    )
    return (
        acceleration.reshape(payload.shape[0], payload.shape[1], 3, -1),
        density_rate.reshape(payload.shape[0], payload.shape[1], -1),
    )


def update(particles, rest_density, acceleration, density_rate):
    gravity_vector = jnp.array([0.0, 0.0, -GRAVITY], jnp.float32)[:, None]
    velocity = particles[:, :, 3:6] + TIME_STEP * (acceleration + gravity_vector)
    position = particles[:, :, 0:3] + TIME_STEP * velocity
    relative = particles[:, :, 6] + TIME_STEP * density_rate / rest_density
    return jnp.concatenate([position, velocity, relative[:, :, None]], axis=2)


def orthonormal(matrix):
    for repeat in range(2):
        inner_product = jnp.dot(matrix.T, matrix, precision=lax.Precision.HIGHEST)
        factor = jnp.linalg.cholesky(inner_product)
        matrix = lax.linalg.triangular_solve(
            factor, matrix, left_side=False, lower=True, transpose_a=True
        )
    return matrix


def pod_weights(gram_matrix, basis_start):
    basis_now = orthonormal(basis_start)
    for iteration in range(POD_ITERS):
        basis_now = orthonormal(jnp.dot(gram_matrix, basis_now, precision=lax.Precision.HIGHEST))
    return jnp.dot(basis_now, basis_now[-1], precision=lax.Precision.HIGHEST)


def extend(payload):
    return with_halo(payload, (("stream", 0), ("vert", 1)), 1)


def advance(particles, rest_density, particle_mass, near_index, cell_shifts):
    payload = make_payload(particles, rest_density, particle_mass)
    extended = extend(payload)
    acceleration, density_rate = interact(payload, extended, near_index, cell_shifts, 4)
    return update(particles, rest_density, acceleration, density_rate)


def body(particles, phase_flags, neighbours, history, basis_start):
    rest_density = 1.0 + SEDIMENT_EXTRA * phase_flags.astype(jnp.float32)
    particle_mass = rest_density * VOLUME
    near_index, cell_shifts = block_layout(neighbours)
    first_state = advance(particles, rest_density, particle_mass, near_index, cell_shifts)
    second_state = advance(first_state, rest_density, particle_mass, near_index, cell_shifts)
    new_snapshots = jnp.stack([first_state[:, :, 3:6], second_state[:, :, 3:6]], axis=3).astype(
        jnp.bfloat16
    )
    snapshots = jnp.concatenate([history, new_snapshots], axis=3)
    gram_matrix = lax.psum(
        jnp.einsum("abcsp,abctp->st", snapshots, snapshots, preferred_element_type=jnp.float32),
        ("stream", "vert"),
    )
    weights = pod_weights(gram_matrix, basis_start)
    filtered = jnp.einsum(
        "abcsp,s->abcp", snapshots.astype(jnp.float32), weights, precision=lax.Precision.HIGHEST
    )
    return (second_state, filtered)


def solution(mesh):
    in_specs = (
        P("stream", "vert", None, None),
        P("stream", "vert", None),
        P("stream", "vert", None),
        P("stream", "vert", None, None, None),
        P(),
    )
    out_specs = (P("stream", "vert", None, None), P("stream", "vert", None, None))
    return jax.shard_map(body, mesh=mesh, in_specs=in_specs, out_specs=out_specs, check_vma=False)
```

profile of v0, /device:TPU:1, one launch (start us, length us, event | category | flops | bytes accessed | tf_op | source)
XLA Modules:
  0.0 584.5 jit_solution(12489457789824271340)
XLA Ops:
  9.6 5.4 collective-permute-start
  15.0 4.7 collective-permute-start.1
  21.8 5.8 %cholesky.164 = f32[64,64]{1,0:T(8,128)S(1)} custom-call(f32[64,64]{1,0:T(8,128)S(1)} %fusion.36), custom_call_target="Cholesky" | custom-call | tf_op jit(solution)/shard_map/jit(cholesky)/cholesky | solution.py:113
  29.0 4.9 custom-call.14
  34.4 5.8 %cholesky.175 = f32[64,64]{1,0:T(8,128)S(1)} custom-call(f32[64,64]{1,0:T(8,128)S(1)} %fusion.34), custom_call_target="Cholesky" | custom-call | tf_op jit(solution)/shard_map/jit(cholesky)/cholesky | solution.py:113
  43.9 1.5 collective-permute-done.2
  45.3 4.2 collective-permute-done.3
  50.5 48.7 %while.24 = (s32[]{:T(128)}, f32[8,4,3,128]{3,2,1,0:T(4,128)S(1)}, f32[8,4,128]{2,1,0:T(4,128)S(1)}, f32[8,4,8,128]{3,1,0,2:T(4,128)S(1)}, s32[8,4,5]{2,1,0:T(4,...) while((s32[]{:T(128)}, f32[8,4,3,128]{3,2,1,0:T(4,128)S(1)}, ...), condition=%wide.region_5.7_spmd, body=%wide.region_0.6_spmd.sunk | while | flops 15424634 | bytes 10094649 | solution.py:88
  50.6 1.6 gather_fusion
  54.1 1.7 multiply_reduce_fusion.15
  56.7 1.6 gather_fusion
  60.2 1.7 multiply_reduce_fusion.15
  62.8 1.6 gather_fusion
  66.3 1.7 multiply_reduce_fusion.15
  68.9 1.6 gather_fusion
  72.3 1.7 multiply_reduce_fusion.15
  75.0 1.6 gather_fusion
  78.4 1.7 multiply_reduce_fusion.15
  81.1 1.6 gather_fusion
  84.5 1.7 multiply_reduce_fusion.15
  87.1 1.6 gather_fusion
  90.6 1.7 multiply_reduce_fusion.15
  93.2 1.6 gather_fusion
  96.7 1.7 multiply_reduce_fusion.15
  100.0 3.7 collective-permute-start.4
  103.7 1.9 collective-permute-start.5
  106.3 4.9 custom-call.15
  111.3 3.1 collective-permute-start.6
  116.7 3.1 copy.166
  123.3 74.8 %while.25 = (s32[]{:T(128)}, f32[8,4,3,128]{3,2,1,0:T(4,128)}, f32[8,4,128]{2,1,0:T(4,128)}, f32[8,4,8,128]{3,1,2,0:T(4,128)}, s32[8,4,5]{2,1,0:T(4,128)}, /*ind...) while((s32[]{:T(128)}, f32[8,4,3,128]{3,2,1,0:T(4,128)}, f32[8,4,128]{2,1,0:T(4,128)}, ...), condition=%wide.region_11.13_spmd, body=%wide.region_6.12_spmd.sunk | while | flops 15424634 | bytes 10093617 | solution.py:88
  124.0 1.6 gather_fusion.1
  128.9 1.8 multiply_reduce_fusion.18
  133.3 1.6 gather_fusion.1
  138.2 1.8 multiply_reduce_fusion.18
  142.7 1.6 gather_fusion.1
  147.5 1.8 multiply_reduce_fusion.18
  152.0 1.6 gather_fusion.1
  156.9 1.8 multiply_reduce_fusion.18
  161.4 1.6 gather_fusion.1
  166.3 1.8 multiply_reduce_fusion.18
  170.8 1.6 gather_fusion.1
  175.6 1.8 multiply_reduce_fusion.18
  180.1 1.6 gather_fusion.1
  185.0 1.8 multiply_reduce_fusion.18
  189.5 1.6 gather_fusion.1
  194.3 1.8 multiply_reduce_fusion.18
  199.1 2.5 fusion.6
  202.5 268.8 %all-reduce.4.cloned.1.call-done = f32[128,128]{1,0:T(8,128)} async-done(((f32[128,128]{1,0:T(8,128)}), f32[128,128]{1,0:T(8,128)}) %all-reduce.4.cloned.1.call-update) | async-done | bytes 65552 | tf_op jit(solution)/shard_map/psum | solution.py:148
  472.7 5.8 %cholesky.186 = f32[64,64]{1,0:T(8,128)S(1)} custom-call(f32[64,64]{1,0:T(8,128)S(1)} %fusion.32), custom_call_target="Cholesky" | custom-call | tf_op jit(solution)/shard_map/jit(cholesky)/cholesky | solution.py:113
  479.9 4.9 custom-call.16
  485.4 5.8 %cholesky.197 = f32[64,64]{1,0:T(8,128)S(1)} custom-call(f32[64,64]{1,0:T(8,128)S(1)} %fusion.30), custom_call_target="Cholesky" | custom-call | tf_op jit(solution)/shard_map/jit(cholesky)/cholesky | solution.py:113
  492.6 4.9 custom-call.17
  499.1 5.8 %cholesky.208 = f32[64,64]{1,0:T(8,128)S(1)} custom-call(f32[64,64]{1,0:T(8,128)S(1)} %fusion.28), custom_call_target="Cholesky" | custom-call | tf_op jit(solution)/shard_map/jit(cholesky)/cholesky | solution.py:113
  506.3 4.9 custom-call.18
  511.7 5.8 %cholesky.219 = f32[64,64]{1,0:T(8,128)S(1)} custom-call(f32[64,64]{1,0:T(8,128)S(1)} %fusion.26), custom_call_target="Cholesky" | custom-call | tf_op jit(solution)/shard_map/jit(cholesky)/cholesky | solution.py:113
  518.9 4.9 custom-call.19
  524.6 5.8 %cholesky.230 = f32[64,64]{1,0:T(8,128)S(1)} custom-call(f32[64,64]{1,0:T(8,128)S(1)} %fusion.24), custom_call_target="Cholesky" | custom-call | tf_op jit(solution)/shard_map/jit(cholesky)/cholesky | solution.py:113
  531.8 4.9 custom-call.20
  537.2 6.0 %cholesky.241 = f32[64,64]{1,0:T(8,128)S(1)} custom-call(f32[64,64]{1,0:T(8,128)S(1)} %fusion.22), custom_call_target="Cholesky" | custom-call | tf_op jit(solution)/shard_map/jit(cholesky)/cholesky | solution.py:113
  544.6 4.9 custom-call.21
  550.3 5.8 %cholesky.252 = f32[64,64]{1,0:T(8,128)S(1)} custom-call(f32[64,64]{1,0:T(8,128)S(1)} %fusion.20), custom_call_target="Cholesky" | custom-call | tf_op jit(solution)/shard_map/jit(cholesky)/cholesky | solution.py:113
  557.4 4.9 custom-call.22
  562.9 5.8 %cholesky.263 = f32[64,64]{1,0:T(8,128)S(1)} custom-call(f32[64,64]{1,0:T(8,128)S(1)} %fusion.18), custom_call_target="Cholesky" | custom-call | tf_op jit(solution)/shard_map/jit(cholesky)/cholesky | solution.py:113
  570.1 4.9 custom-call.23
  (521 shorter events, 107.7 us)
Async XLA Ops:
  7.2 14.3 %copy-start = (f32[128,64]{0,1:T(8,128)S(1)}, f32[128,64]{0,1:T(8,128)}, u32[]{:S(2)}) copy-start(f32[128,64]{0,1:T(8,128)} %param.20) | copy-start | bytes 98308
  7.2 464.1 %all-reduce.4.cloned.1.call-start = ((), (), s32[]{:S(2)}) async-start(), calls=%async_computation | async-start | bytes 131072 | tf_op jit(solution)/shard_map/psum | solution.py:148
  9.6 30.8 %collective-permute-start = (f32[1,1,8,128]{3,0,2,1:T(1,128)S(1)}, f32[1,1,8,128]{3,0,2,1:T(1,128)S(1)}, u32[]{:S(2)}, u32[]{:S(2)}) collective-permute-start(f32[1,1,8,128]{3,0,2,1:T(1,128)S(1)} %get-tuple-element.168), channel_id=1, source_target_pairs={{0,4},{4,8},{8,12},{12,16},{16,20},{20,24},{24,28},{28,32},{32,36}... | collective-permute-start | bytes 12296 | tf_op jit(solution)/shard_map/ppermute | solution.py:24
  15.0 25.4 %collective-permute-start.1 = (f32[1,1,8,128]{3,0,2,1:T(1,128)S(1)}, f32[1,1,8,128]{3,0,2,1:T(1,128)S(1)}, u32[]{:S(2)}, u32[]{:S(2)}) collective-permute-start(f32[1,1,8,128]{3,0,2,1:T(1,128)S(1)} %get-tuple-element.169), channel_id=1, source_target_pairs={{4,0},{8,4},{12,8},{16,12},{20,16},{24,20},{28,24},{32,28},{36,32}... | collective-permute-start | bytes 12296 | tf_op jit(solution)/shard_map/ppermute | solution.py:27
  40.5 4.9 collective-permute-start.2
  41.8 7.8 %collective-permute-start.3 = (f32[34,1,8,128]{3,0,2,1:T(8,128)S(1)}, f32[34,1,8,128]{3,0,2,1:T(8,128)S(1)}, u32[]{:S(2)}, u32[]{:S(2)}) collective-permute-start(f32[34,1,8,128]{3,0,2,1:T(8,128)S(1)} %pad_maximum_fusion.2), channel_id=1, source_target_pairs={{1,0},{2,1},{3,2},{5,4},{6,5},{7,6},{9,8},{10,9},{11,10},{13,12},{... | collective-permute-start | bytes 417800 | tf_op jit(solution)/shard_map/ppermute | solution.py:27
  50.5 48.8 %copy-start.3 = (s32[32,1,128]{2,1,0:T(1,128)S(1)}, s32[32,1,128]{2,1,0:T(1,128)}, u32[]{:S(2)}) copy-start(s32[32,1,128]{2,1,0:T(1,128)} %param.17) | copy-start | bytes 49156
  50.5 49.4 %copy-start.10 = (f32[3]{0:T(128)S(1)}, f32[3]{0:T(128)}, u32[]{:S(2)}) copy-start(f32[3]{0:T(128)} %constant.134.clone) | copy-start | bytes 40
  99.2 0.6 copy-start.2
  99.2 16.7 %copy-start.7 = (s32[8,4,5]{2,1,0:T(4,128)}, s32[8,4,5]{2,1,0:T(4,128)S(1)}, u32[]{:S(2)}) copy-start(s32[8,4,5]{2,1,0:T(4,128)S(1)} %get-tuple-element.364) | copy-start | bytes 1924
  99.2 0.6 copy-start.4
  100.0 11.2 %collective-permute-start.4 = (f32[1,1,8,128]{3,2,1,0:T(8,128)S(1)}, f32[1,1,8,128]{3,2,1,0:T(8,128)S(1)}, u32[]{:S(2)}, u32[]{:S(2)}) collective-permute-start(f32[1,1,8,128]{3,2,1,0:T(8,128)S(1)} %get-tuple-element.166), channel_id=1, source_target_pairs={{0,4},{4,8},{8,12},{12,16},{16,20},{20,24},{24,28},{28,32},{32,36}... | collective-permute-start | bytes 12296 | tf_op jit(solution)/shard_map/ppermute | solution.py:24
  103.7 7.5 %collective-permute-start.5 = (f32[1,1,8,128]{3,2,1,0:T(8,128)S(1)}, f32[1,1,8,128]{3,2,1,0:T(8,128)S(1)}, u32[]{:S(2)}, u32[]{:S(2)}) collective-permute-start(f32[1,1,8,128]{3,2,1,0:T(8,128)S(1)} %get-tuple-element.167), channel_id=1, source_target_pairs={{4,0},{8,4},{12,8},{16,12},{20,16},{24,20},{28,24},{32,28},{36,32}... | collective-permute-start | bytes 12296 | tf_op jit(solution)/shard_map/ppermute | solution.py:27
  111.3 9.9 %collective-permute-start.6 = (f32[34,1,8,128]{3,2,1,0:T(8,128)S(1)}, f32[34,1,8,128]{3,2,1,0:T(8,128)S(1)}, u32[]{:S(2)}, u32[]{:S(2)}) collective-permute-start(f32[34,1,8,128]{3,2,1,0:T(8,128)S(1)} %pad_maximum_fusion.3), channel_id=1, source_target_pairs={{0,1},{1,2},{2,3},{4,5},{5,6},{6,7},{8,9},{9,10},{10,11},{12,13},{... | collective-permute-start | bytes 417800 | tf_op jit(solution)/shard_map/ppermute | solution.py:24
  114.4 6.8 %collective-permute-start.7 = (f32[34,1,8,128]{3,2,1,0:T(8,128)S(1)}, f32[34,1,8,128]{3,2,1,0:T(8,128)S(1)}, u32[]{:S(2)}, u32[]{:S(2)}) collective-permute-start(f32[34,1,8,128]{3,2,1,0:T(8,128)S(1)} %pad_maximum_fusion.3), channel_id=1, source_target_pairs={{1,0},{2,1},{3,2},{5,4},{6,5},{7,6},{9,8},{10,9},{11,10},{13,12},{... | collective-permute-start | bytes 417800 | tf_op jit(solution)/shard_map/ppermute | solution.py:27
  199.0 2.6 copy-start.8
  199.0 2.6 copy-start.5
  199.1 272.2 %copy-start.6 = (f32[128,64]{0,1:T(8,128)S(1)}, f32[128,64]{0,1:T(8,128)}, u32[]{:S(2)}) copy-start(f32[128,64]{0,1:T(8,128)} %convolution_bitcast_fusion.8) | copy-start | bytes 98308
  471.3 52.8 %copy-start.1 = (f32[128,128]{1,0:T(8,128)S(1)}, f32[128,128]{1,0:T(8,128)}, u32[]{:S(2)}) copy-start(f32[128,128]{1,0:T(8,128)} %all-reduce.4.cloned.1.call-done) | copy-start | bytes 196612
  511.4 64.1 %copy-start.9 = (bf16[32,1,3,1,128]{4,3,2,0,1:T(2,128)(2,1)S(1)}, bf16[32,1,3,1,128]{4,3,2,0,1:T(2,128)(2,1)}, u32[]{:S(2)}) copy-start(bf16[32,1,3,1,128]{4,3,2,0,1:T(2,128)(2,1)} %copy.167) | copy-start | bytes 73732
Sparse Core Ops, SparseCore 0:
  201.7 269.5 all-reduce.3
where the time goes:
time: 587 us; the launch traced here: 584 us
  waiting for transfers between devices  275 us (47%)
  other arithmetic  200 us (34%)
  local copies, waits for them, and re-layouts  58.8 us (10%)
  starting transfers between devices  22.9 us (4%)
  between operations  14.9 us (3%)
  matrix products  11.6 us (2%)
    psum x1, waiting for transfers between devices, body(): lax.psum(jnp.einsum('abcsp,abctp->st', snapshots, snapshots, preferred_el...  269 us
    another operation x30, other arithmetic, orthonormal(): factor = jnp.linalg.cholesky(inner_product)  65.3 us
    another operation x20, other arithmetic, orthonormal(): lax.linalg.triangular_solve(factor, matrix, left_side=False, lower=True,...  55.5 us
    reduce_sum x16, other arithmetic, forces(): jnp.sum(closing * separation, axis=2)  28.4 us
    gather x16, local copies, waits for them, and re-layouts, one_group(): near_blocks = jnp.take(flat_blocks, index_part, axis=0)  25 us
    ppermute x4, starting transfers between devices, with_halo(): lax.ppermute(lax.slice_in_dim(block, block.shape[dim] - width, None, axis...  13.5 us
    reduce_sum x16, other arithmetic, forces(): radius = jnp.sqrt(jnp.sum(separation * separation, axis=2))  11.9 us
  transfers between devices with their start and end apart: 9, of which 3 were waited for; matrix products, arithmetic and copies ran while one was open for 6% of the time, Pallas kernels for 0%

commit v1 on v0

v1 whole, which is shorter than its diff:
```python
import functools
import math

import jax
import jax.numpy as jnp
from jax import lax
from jax.experimental import pallas as pl
from jax.experimental.pallas import tpu as pltpu
from jax.sharding import PartitionSpec as P

POD_ITERS = 4
VOLUME = 1.0 / 16.0
STIFFNESS = 100.0 / 7.0
SLOPE = -5.0 * 21.0 / (16.0 * math.pi)
DT = 0.02
SEDIMENT_EXTRA = 1.65

HI = lax.Precision.HIGHEST
NT = (((1,), (1,)), ((), ()))
NN = (((1,), (0,)), ((), ()))
TN = (((0,), (0,)), ((), ()))
BF = jnp.bfloat16
F32 = jnp.float32
MESH = pl.DeviceIdType.MESH
VM = pl.BlockSpec(memory_space=pltpu.VMEM)

def split3(x):
    a = x.astype(BF).astype(F32)
    b = (x - a).astype(BF).astype(F32)
    return a, b, x - a - b


def forces_kernel(codes_ref, ext_ref, relative_ref, out_ref, next_ref):
    blocks = relative_ref.shape[0]
    part = relative_ref.shape[-1]
    row = lax.broadcasted_iota(jnp.int32, (8, part), 0)

    def centred(vert, stream, ds, dv):
        field = ext_ref[vert, stream]
        shift = jnp.where(row == 0, 2.0 * ds - 1.0, jnp.where(row == 1, -1.0, jnp.where(row == 2, 2.0 * dv - 1.0, 0.0)))
        return field + shift

    def norm(half):
        square = half * half
        return square[0:1] + square[1:2] + square[2:3]

    def one_block(b, carry):
        own = centred(1, b + 1, 0.0, 0.0)
        half = 0.5 * own
        target = jnp.where(row < 3, half, jnp.where(row == 3, 1.0, jnp.where(row == 4, norm(half), 0.0)))
        h, m, l = split3(target)
        target = jnp.concatenate([h, h, m, h, l, m], axis=0).astype(BF)
        sums = jnp.zeros((16, part), F32)
        for n in range(5):
            if n == 0:
                vert, stream, ds, dv = 1, b + 1, 0.0, 0.0
            else:
                code = codes_ref[b, n - 1]
                code = jnp.where(code >= 4, code + 1, code)
                third = lax.div(code, 3)
                ds, dv = third - 1, code - 3 * third - 1
                vert, stream = dv + 1, b + 1 + ds
                ds, dv = ds.astype(F32), dv.astype(F32)
            near = centred(vert, stream, ds, dv)
            half = 0.5 * near
            source = jnp.where(row < 3, -2.0 * half, jnp.where(row == 3, norm(half), jnp.where(row == 4, 1.0, 0.0)))
            h, m, l = split3(source)
            source = jnp.concatenate([h, m, h, l, h, m], axis=0).astype(BF)
            mass = near[6:7]
            weighted = jnp.where(row == 6, 1.0, near) * mass
            dots = near[0:3] * near[3:6]
            dot = mass * (dots[0:1] + dots[1:2] + dots[2:3])
            second = jnp.where(row < 3, weighted * near[7:8], jnp.where(row == 3, dot, 0.0))
            fields = jnp.concatenate([weighted, second], axis=0)
            high = fields.astype(BF)
            low = (fields - high.astype(F32)).astype(BF)
            quarter = lax.dot_general(target, source, TN, preferred_element_type=F32)
            quarter = jnp.maximum(quarter, 1e-30)
            reach = jnp.maximum(1.0 - quarter * lax.rsqrt(quarter), 0.0)
            cube = reach * reach * reach
            cube_high = cube.astype(BF)
            cube_low = (cube - cube_high.astype(F32)).astype(BF)
            part_a = lax.dot_general(jnp.concatenate([high, low], axis=0), cube_high, NT, preferred_element_type=F32)
            part_b = lax.dot_general(high, cube_low, NT, preferred_element_type=F32)
            sums = sums + (part_a[0:16] + part_a[16:32] + part_b)
        relative = relative_ref[b]
        density = 16.0 * own[6:7]
        place, speed, pressure = own[0:3], own[3:6], own[7:8]
        total, pressure_total, vx = sums[6:7], sums[7:8], sums[11:12]
        dots = speed * (place * total - sums[0:3]) - place * sums[3:6]
        rate = SLOPE * (dots[0:1] + dots[1:2] + dots[2:3] + vx)
        acc = -SLOPE * (pressure * (place * total - sums[0:3]) + place * pressure_total - sums[8:11])
        gravity = jnp.where(row[0:3] == 2, -1.0, 0.0)
        speed = speed + DT * (acc + gravity)
        place = ext_ref[1, b + 1][0:3] + DT * speed
        relative = relative + DT * rate / density
        power = relative * relative
        power = power * power * power * relative
        pressure = STIFFNESS * (power - 1.0) / (density * relative * relative)
        out_ref[b] = jnp.concatenate([place, speed, relative], axis=0)
        next_ref[b] = jnp.concatenate([place, speed, own[6:7], pressure], axis=0)
        return carry

    lax.fori_loop(0, blocks, one_block, 0)


def forces_step(codes, ext, relative):
    blocks, _, part = relative.shape
    vm = pl.BlockSpec(memory_space=pltpu.VMEM)
    return pl.pallas_call(
        forces_kernel,
        out_shape=(jax.ShapeDtypeStruct((blocks, 7, part), F32), jax.ShapeDtypeStruct((blocks, 8, part), F32)),
        in_specs=[pl.BlockSpec(memory_space=pltpu.SMEM), vm, vm],
        out_specs=(vm, vm),
        name="forces",
    )(codes, ext, relative)

def orthonormal_rows(t):
    rank, width = t.shape
    zero = jnp.zeros((width - rank, width), jnp.float32)
    lane = lax.broadcasted_iota(jnp.int32, (rank, width), 1)
    row = lax.broadcasted_iota(jnp.int32, (rank, width), 0)
    unit = jnp.where(lane == row + rank, 1.0, 0.0)
    work = lax.dot_general(t, jnp.concatenate([t, zero], axis=0), NT, precision=HI) + unit
    eight = lax.broadcasted_iota(jnp.int32, (8, width), 0)
    count = rank // 8

    def panel(p, groups):
        groups = list(groups)
        cols = [
            [jnp.where(g + p < count, jnp.broadcast_to(groups[g][:, c:c + 1], (8, width)), 0.0) for g in range(count)]
            for c in range(8)
        ]
        for k in range(8):
            inv = lax.rsqrt(jnp.broadcast_to(cols[k][0][k:k + 1], (8, width)))
            low = [cols[k][g] * inv for g in range(count)]
            pivot_row = jnp.broadcast_to(groups[0][k:k + 1], (8, width)) * inv
            for c in range(k + 1, 8):
                factor = jnp.broadcast_to(low[0][c:c + 1], (8, width))
                for g in range(count):
                    cols[c][g] = cols[c][g] - low[g] * factor
            groups[0] = jnp.where(eight == k, pivot_row, jnp.where(eight > k, groups[0] - low[0] * pivot_row, groups[0]))
            for g in range(1, count):
                groups[g] = groups[g] - low[g] * pivot_row
        groups = groups[1:] + groups[:1]
        return tuple(pltpu.roll(x, width - 8, 1) for x in groups)

    groups = lax.fori_loop(0, count, panel, tuple(work[8 * g:8 * g + 8] for g in range(count)))
    done = jnp.concatenate(groups, axis=0)
    return lax.dot_general(done, jnp.concatenate([t, zero], axis=0), NN, precision=HI)
def pod_kernel(iters, gram_ref, start_ref, out_ref):
    def half(i, t):
        t = orthonormal_rows(t)
        again = jnp.logical_and(i % 2 == 1, i < 2 * iters + 1)
        return lax.cond(
            again,
            lambda t: lax.dot_general(t, gram_ref[...], NN, precision=HI),
            lambda t: t,
            t,
        )

    t = lax.fori_loop(0, 2 * iters + 2, half, start_ref[...])
    last = jnp.broadcast_to(t[:, -1:], t.shape)
    out_ref[...] = jnp.broadcast_to(jnp.sum(t * last, axis=0, keepdims=True), out_ref.shape)


def pod_weights(gram, start_t, iters=POD_ITERS):
    return pl.pallas_call(
        functools.partial(pod_kernel, iters),
        out_shape=jax.ShapeDtypeStruct((8, gram.shape[0]), jnp.float32),
        in_specs=[pl.BlockSpec(memory_space=pltpu.VMEM)] * 2,
        out_specs=pl.BlockSpec(memory_space=pltpu.VMEM),
        name="pod",
    )(gram, start_t)

SIDES = [(ds, dv) for dv in (-1, 0, 1) for ds in (-1, 0, 1) if (ds, dv) != (0, 0)]


def halo_kernel(own_ref, ext_ref, local_sem, send_sem, recv_sem):
    blocks = own_ref.shape[0]
    streams, verts = lax.axis_size("stream"), lax.axis_size("vert")
    me_s, me_v = lax.axis_index("stream"), lax.axis_index("vert")

    def present(ds, dv):
        s, v = me_s + ds, me_v + dv
        return jnp.logical_and(jnp.logical_and(s >= 0, s < streams), jnp.logical_and(v >= 0, v < verts))

    def rows(ds, start):
        if ds == 0:
            return pl.ds(start, blocks)
        return None

    def copy(index):
        ds, dv = SIDES[index]
        if ds == 0:
            source, target = own_ref, ext_ref.at[1 - dv, pl.ds(1, blocks)]
        elif ds == 1:
            source, target = own_ref.at[pl.ds(blocks - 1, 1)], ext_ref.at[1 - dv, pl.ds(0, 1)]
        else:
            source, target = own_ref.at[pl.ds(0, 1)], ext_ref.at[1 - dv, pl.ds(blocks + 1, 1)]
        return pltpu.make_async_remote_copy(
            src_ref=source,
            dst_ref=target,
            send_sem=send_sem.at[index],
            recv_sem=recv_sem.at[index],
            device_id=(me_s + ds, me_v + dv),
            device_id_type=MESH,
        )

    local = pltpu.make_async_copy(own_ref, ext_ref.at[1, pl.ds(1, blocks)], local_sem)
    local.start()
    barrier = pltpu.get_barrier_semaphore()
    count = 0
    for ds, dv in SIDES:
        here = present(ds, dv)
        count = count + here.astype(jnp.int32)

        @pl.when(here)
        def _():
            pl.semaphore_signal(barrier, inc=1, device_id=(me_s + ds, me_v + dv), device_id_type=MESH)

    pl.semaphore_wait(barrier, count)
    for index, (ds, dv) in enumerate(SIDES):

        @pl.when(present(ds, dv))
        def _():
            copy(index).start()

        @pl.when(jnp.logical_not(present(ds, dv)))
        def _():
            if ds == 0:
                ext_ref[1 + dv, 1 : blocks + 1] = jnp.zeros(own_ref.shape, F32)
            else:
                ext_ref[1 + dv, 0 if ds < 0 else blocks + 1] = jnp.zeros(own_ref.shape[1:], F32)

    for index, (ds, dv) in enumerate(SIDES):
        back = SIDES.index((-ds, -dv))

        @pl.when(present(ds, dv))
        def _():
            copy(index).wait_send()
            copy(back).wait_recv()

    local.wait()


def halo(payload, collective_id):
    blocks, fields, part = payload.shape
    return pl.pallas_call(
        halo_kernel,
        out_shape=jax.ShapeDtypeStruct((3, blocks + 2, fields, part), F32),
        in_specs=[VM],
        out_specs=VM,
        scratch_shapes=[
            pltpu.SemaphoreType.DMA,
            pltpu.SemaphoreType.DMA((8,)),
            pltpu.SemaphoreType.DMA((8,)),
        ],
        compiler_params=pltpu.CompilerParams(collective_id=collective_id, has_side_effects=True),
        name="halo",
    )(payload)


LONG = 8


def reduce_kernel(gram_ref, out_ref, slots, sums, send_sem, recv_sem):
    stream, vert = lax.axis_index("stream"), lax.axis_index("vert")
    core, z, y = stream % 2, (stream // 2) % LONG, stream // (2 * LONG)
    near = vert * 2 + core
    size = gram_ref.shape[0] // LONG

    def near_device(r):
        return (stream - core + r % 2, r // 2)

    def z_device(r):
        return (stream + (r - z) * 2, vert)

    def y_device(r):
        return (stream + (r - y) * 2 * LONG, vert)

    barrier = pltpu.get_barrier_semaphore()
    for me, device in ((near, near_device), (z, z_device), (y, y_device)):
        for step in range(1, LONG):
            pl.semaphore_signal(barrier, inc=1, device_id=device((me + step) % LONG), device_id_type=MESH)
    pl.semaphore_wait(barrier, 3 * (LONG - 1))

    def exchange(stage, me, device, source, target):
        def copy(step):
            other = (me + step) % LONG
            return pltpu.make_async_remote_copy(
                src_ref=source(other),
                dst_ref=target(step),
                send_sem=send_sem.at[stage, step],
                recv_sem=recv_sem.at[stage, step],
                device_id=device(other),
                device_id_type=MESH,
            )

        for step in range(1, LONG):
            copy(step).start()
        for step in range(1, LONG):
            copy(step).wait()

    def total(stage, own):
        for step in range(1, LONG):
            own = own + slots[stage, step]
        return own

    mine = pl.ds(pl.multiple_of(near * size, size), size)
    exchange(
        0, near, near_device,
        lambda other: gram_ref.at[pl.ds(pl.multiple_of(other * size, size), size)],
        lambda step: slots.at[0, step],
    )
    sums[0] = total(0, gram_ref[mine])
    exchange(1, z, z_device, lambda other: sums.at[0], lambda step: slots.at[1, step])
    sums[1] = total(1, sums[0])
    exchange(2, y, y_device, lambda other: sums.at[1], lambda step: slots.at[2, step])
    sums[2] = total(2, sums[1])
    out_ref[mine] = sums[2]
    exchange(3, near, near_device, lambda other: sums.at[2], lambda step: out_ref.at[mine])


def reduce_gram(gram, collective_id):
    size = gram.shape[0] // LONG
    return pl.pallas_call(
        reduce_kernel,
        out_shape=jax.ShapeDtypeStruct(gram.shape, F32),
        in_specs=[VM],
        out_specs=VM,
        scratch_shapes=[
            pltpu.VMEM((3, LONG, size, gram.shape[1]), F32),
            pltpu.VMEM((3, size, gram.shape[1]), F32),
            pltpu.SemaphoreType.DMA((4, LONG)),
            pltpu.SemaphoreType.DMA((4, LONG)),
        ],
        compiler_params=pltpu.CompilerParams(collective_id=collective_id, has_side_effects=True),
        name="reduce",
    )(gram)


def body(particles, phase_flags, neighbours, history, basis_start):
    state = particles[:, 0]
    codes = neighbours[:, 0]
    rest_density = 1.0 + SEDIMENT_EXTRA * phase_flags.astype(F32)
    mass = rest_density * VOLUME
    relative = state[:, 6:7]
    pressure = STIFFNESS * (relative**7 - 1.0) / (rest_density * relative * relative)
    payload = jnp.concatenate([state[:, 0:6], mass, pressure], axis=1)
    first, payload = forces_step(codes, halo(payload, 0), relative)
    second, _ = forces_step(codes, halo(payload, 1), first[:, 6:7])
    newest = jnp.stack([first[:, 3:6], second[:, 3:6]], axis=2).astype(BF)
    snapshots = jnp.concatenate([history[:, 0], newest], axis=2)
    gram = jnp.einsum("acsp,actp->st", snapshots, snapshots, preferred_element_type=F32)
    weights = pod_weights(reduce_gram(gram, 2), basis_start.T)[0]
    filtered = jnp.einsum("acsp,s->acp", snapshots.astype(F32), weights, precision=HI)
    return (second[:, None], filtered[:, None])


def solution(mesh):
    in_specs = (
        P("stream", "vert", None, None),
        P("stream", "vert", None),
        P("stream", "vert", None),
        P("stream", "vert", None, None, None),
        P(),
    )
    out_specs = (P("stream", "vert", None, None), P("stream", "vert", None, None))
    return jax.shard_map(body, mesh=mesh, in_specs=in_specs, out_specs=out_specs, check_vma=False)
```

time: 587 us -> 171 us (0.29)
  waiting for transfers between devices: 275 us -> 0 us
  other arithmetic: 200 us -> 2.1 us
  Pallas kernels: 0 us -> 152 us
  local copies, waits for them, and re-layouts: 58.8 us -> 11.2 us
  starting transfers between devices: 22.9 us -> 0 us
  between operations: 14.9 us -> 0.69 us
  matrix products: 11.6 us -> 3.63 us
    psum x1 -> x0, waiting for transfers between devices: 269 us -> none  [body(): lax.psum(jnp.einsum('abcsp,abctp->st', snapshots, snapshots, preferred_el...]
    pallas_call x0 -> x6, Pallas kernels: none -> 152 us  [the longest x2 72.7 us: forces_step(): pl.pallas_call(forces_kernel, out_shape=(jax.ShapeDtypeStruct((blocks, 7,...]
    another operation x53 -> x0, other arithmetic: 122 us -> none  [the longest x30 65.3 us: orthonormal(): factor = jnp.linalg.cholesky(inner_product)]
    reduce_sum x48 -> x0, other arithmetic: 51.9 us -> none  [the longest x16 28.4 us: forces(): jnp.sum(closing * separation, axis=2)]
    gather x16 -> x0, local copies, waits for them, and re-layouts: 25 us -> none  [one_group(): near_blocks = jnp.take(flat_blocks, index_part, axis=0)]
    ppermute x8 -> x0, starting transfers between devices: 22.8 us -> none  [the longest x4 13.5 us: with_halo(): lax.ppermute(lax.slice_in_dim(block, block.shape[dim] - width, None, axis...]
    mul x35 -> x1, other arithmetic: 10.7 us -> 0.73 us  [body(): rest_density = 1.0 + SEDIMENT_EXTRA * phase_flags.astype(F32)]
    sub x32 -> x0, local copies, waits for them, and re-layouts: 7.42 us -> none  [forces(): own_block[:, None, 0:3, :, None] - near_blocks[:, :, 0:3, None, :]]
  transfers between devices with their start and end apart: 9 -> 0, of which waited for: 3 -> 0; matrix products, arithmetic and copies ran while one was open for 6% -> 0% of each run, Pallas kernels for 0% -> 0%
where the time goes in v1:
time: 171 us; the launch traced here: 170 us
  Pallas kernels  152 us (89%)
  local copies, waits for them, and re-layouts  11.2 us (7%)
  matrix products  3.63 us (2%)
  other arithmetic  2.1 us (1%)
    pallas_call x2, Pallas kernels, forces_step(): pl.pallas_call(forces_kernel, out_shape=(jax.ShapeDtypeStruct((blocks, 7,...  72.7 us
    pallas_call x1, Pallas kernels, reduce_gram(): pl.pallas_call(reduce_kernel, out_shape=jax.ShapeDtypeStruct(gram.shape,...  29.8 us
    pallas_call x1, Pallas kernels, pod_weights(): pl.pallas_call(functools.partial(pod_kernel, iters), out_shape=jax.ShapeD...  26.4 us
    pallas_call x2, Pallas kernels, halo(): pl.pallas_call(halo_kernel, out_shape=jax.ShapeDtypeStruct((3, blocks + 2...  23.6 us
    unnamed x3, local copies, waits for them, and re-layouts  5.42 us

profile of v1, /device:TPU:1, one launch (start us, length us, event | category | flops | bytes accessed | tf_op | source)
XLA Modules:
  0.0 170.1 jit_solution(3373952707286558938)
XLA Ops:
  0.6 1.4 copy.30.codes_ref
  2.0 0.7 convert_multiply_fusion
  2.7 0.9 copy.45
  3.6 0.7 fusion.13
  4.3 0.7 pad_maximum_fusion.5.own_ref
  5.0 15.0 %halo.2.ext_ref = f32[3,34,8,128]{3,2,1,0:T(8,128)} custom-call(f32[32,8,128]{2,1,0:T(8,128)} %pad_maximum_fusion.5.own_ref), custom_call_target="tpu_custom_call" | custom-call | tf_op jit(solution)/shard_map/halo/pallas_call | solution.py:249
  20.0 36.3 %forces.2 = (f32[32,7,128]{2,1,0:T(8,128)}, f32[32,8,128]{2,1,0:T(8,128)}) custom-call(s32[32,4]{1,0:T(8,128)} %copy.30.codes_ref, f32[3,34,8,128]{3,2,1,0:T(8,128)} %halo.2.ext_ref, f32[32,1,128]{2,1,0:T(1,128)} %get-tuple-element.14.relative_ref), custom_call_target="tpu_custom_call" | custom-call | tf_op jit(solution)/shard_map/forces/pallas_call | solution.py:110
  56.3 1.5 slice.22.relative_ref
  57.9 0.9 fusion.3
  58.9 8.6 %halo.3.ext_ref = f32[3,34,8,128]{3,2,1,0:T(8,128)} custom-call(f32[32,8,128]{2,1,0:T(8,128)} %get-tuple-element.5.own_ref), custom_call_target="tpu_custom_call" | custom-call | tf_op jit(solution)/shard_map/halo/pallas_call | solution.py:249
  67.4 36.3 %forces.3 = (f32[32,7,128]{2,1,0:T(8,128)}, f32[32,8,128]{2,1,0:T(8,128)}) custom-call(s32[32,4]{1,0:T(8,128)} %copy.30.codes_ref, f32[3,34,8,128]{3,2,1,0:T(8,128)} %halo.3.ext_ref, f32[32,1,128]{2,1,0:T(1,128)} %slice.22.relative_ref), custom_call_target="tpu_custom_call" | custom-call | tf_op jit(solution)/shard_map/forces/pallas_call | solution.py:110
  103.8 0.9 fusion.4
  104.8 1.7 copy.34
  106.4 3.1 %copy.44 = bf16[32,1,3,126,128]{4,3,2,0,1:T(8,128)(2,1)S(1)} copy(bf16[32,1,3,126,128]{4,0,3,2,1:T(8,128)(2,1)} %param.8) | data formatting | bytes 6193152 | tf_op args[3]
  109.5 1.6 fusion.2.gram_ref
  111.1 29.8 %reduce.1.gram_ref = f32[128,128]{1,0:T(8,128)} custom-call(f32[128,128]{1,0:T(8,128)} %fusion.2.gram_ref), custom_call_target="tpu_custom_call" | custom-call | tf_op jit(solution)/shard_map/reduce/pallas_call | solution.py:327
  140.9 26.4 %pod.1 = f32[8,128]{1,0:T(8,128)} custom-call(f32[128,128]{1,0:T(8,128)} %reduce.1.gram_ref, f32[64,128]{1,0:T(8,128)} %bitcast.42), custom_call_target="tpu_custom_call" | custom-call | tf_op jit(solution)/shard_map/pod/pallas_call | solution.py:168
  167.4 2.0 %fusion = f32[1,32,3,128]{3,0,2,1:T(1,128)S(1)} fusion(bf16[32,3,1,128]{3,2,1,0:T(2,128)(2,1)S(1)} %copy.33, bf16[32,3,1,128]{3,2,1,0:T(2,128)(2,1)S(1)} %copy.32, bf16[32,3,126,128]{3,2,1,0:T(8,128)(2,1)S(1)} %bitcast.35, f32[8,128]{1,0:T(8,128)} %pod.1), kind=kOutput, calls=%fused_computation.2 | convolution fusion | flops 28311552 | bytes 3195392 | tf_op jit(solution)/shard_map/acsp,s->acp/dot_general | solution.py:357
  169.4 0.7 copy.35
  (4 shorter events, 0.1 us)

commit v2 on v1

--- a/solution.py
+++ b/solution.py
@@ -50,7 +50,7 @@
         target = jnp.where(row < 3, half, jnp.where(row == 3, 1.0, jnp.where(row == 4, norm(half), 0.0)))
         h, m, l = split3(target)
         target = jnp.concatenate([h, h, m, h, l, m], axis=0).astype(BF)
-        sums = jnp.zeros((16, part), F32)
+        lefts, rights = [], []
         for n in range(5):
             if n == 0:
                 vert, stream, ds, dv = 1, b + 1, 0.0, 0.0
@@ -80,9 +80,13 @@
             cube = reach * reach * reach
             cube_high = cube.astype(BF)
             cube_low = (cube - cube_high.astype(F32)).astype(BF)
-            part_a = lax.dot_general(jnp.concatenate([high, low], axis=0), cube_high, NT, preferred_element_type=F32)
-            part_b = lax.dot_general(high, cube_low, NT, preferred_element_type=F32)
-            sums = sums + (part_a[0:16] + part_a[16:32] + part_b)
+            left = jnp.concatenate([cube_high, cube_low], axis=1)
+            right = jnp.concatenate([jnp.concatenate([high, high], axis=1), jnp.concatenate([low, jnp.zeros_like(low)], axis=1)], axis=0)
+            lefts.append(left)
+            rights.append(right)
+        sums = lax.dot_general(jnp.concatenate(lefts, axis=1), jnp.concatenate(rights, axis=1), NT, preferred_element_type=F32)
+        sums = jnp.transpose(sums)
+        sums = sums[0:16] + sums[16:32]
         relative = relative_ref[b]
         density = 16.0 * own[6:7]
         place, speed, pressure = own[0:3], own[3:6], own[7:8]
@@ -101,7 +105,12 @@
         next_ref[b] = jnp.concatenate([place, speed, own[6:7], pressure], axis=0)
         return carry
 
-    lax.fori_loop(0, blocks, one_block, 0)
+    def several(i, carry):
+        for k in range(4):
+            one_block(4 * i + k, carry)
+        return carry
+
+    lax.fori_loop(0, blocks // 4, several, 0)
 
 
 def forces_step(codes, ext, relative):

time: 171 us -> 120 us (0.70)
  Pallas kernels: 152 us -> 102 us
    pallas_call x2, Pallas kernels: 72.7 us -> 21.9 us  [forces_step(): pl.pallas_call(forces_kernel, out_shape=(jax.ShapeDtypeStruct((blocks, 7,...]
where the time goes in v2:
time: 120 us; the launch traced here: 119 us
  Pallas kernels  102 us (85%)
  local copies, waits for them, and re-layouts  11.2 us (9%)
  matrix products  3.63 us (3%)
  other arithmetic  2.1 us (2%)
    pallas_call x1, Pallas kernels, reduce_gram(): pl.pallas_call(reduce_kernel, out_shape=jax.ShapeDtypeStruct(gram.shape,...  29.9 us
    pallas_call x1, Pallas kernels, pod_weights(): pl.pallas_call(functools.partial(pod_kernel, iters), out_shape=jax.ShapeD...  26.4 us
    pallas_call x2, Pallas kernels, halo(): pl.pallas_call(halo_kernel, out_shape=jax.ShapeDtypeStruct((3, blocks + 2...  23.6 us
    pallas_call x2, Pallas kernels, forces_step(): pl.pallas_call(forces_kernel, out_shape=(jax.ShapeDtypeStruct((blocks, 7,...  21.9 us
    unnamed x3, local copies, waits for them, and re-layouts  5.42 us

profile of v2, /device:TPU:1, one launch (start us, length us, event | category | flops | bytes accessed | tf_op | source)
XLA Modules:
  0.0 119.3 jit_solution(6272236262408061038)
XLA Ops:
  0.6 1.4 %copy.30.codes_ref = s32[32,4]{1,0:T(8,128)} copy(s32[32,4]{0,1:T(4,128)} %bitcast.44) | data formatting | bytes 1024 | tf_op jit(solution)/shard_map/squeeze | solution.py:354
  2.0 0.7 convert_multiply_fusion
  2.7 0.9 copy.45
  3.6 0.7 fusion.13
  4.3 0.7 pad_maximum_fusion.5.own_ref
  5.0 15.0 %halo.2.ext_ref = f32[3,34,8,128]{3,2,1,0:T(8,128)} custom-call(f32[32,8,128]{2,1,0:T(8,128)} %pad_maximum_fusion.5.own_ref), custom_call_target="tpu_custom_call" | custom-call | tf_op jit(solution)/shard_map/halo/pallas_call | solution.py:258
  20.0 11.0 %forces.2 = (f32[32,7,128]{2,1,0:T(8,128)}, f32[32,8,128]{2,1,0:T(8,128)}) custom-call(s32[32,4]{1,0:T(8,128)} %copy.30.codes_ref, f32[3,34,8,128]{3,2,1,0:T(8,128)} %halo.2.ext_ref, f32[32,1,128]{2,1,0:T(1,128)} %get-tuple-element.14.relative_ref), custom_call_target="tpu_custom_call" | custom-call | tf_op jit(solution)/shard_map/forces/pallas_call | solution.py:119
  31.0 1.5 %slice.22.relative_ref = f32[32,1,128]{2,1,0:T(1,128)} slice(f32[32,7,128]{2,1,0:T(8,128)} %get-tuple-element.6), slice={[0:32], [6:7], [0:128]} | slice | bytes 32768 | tf_op jit(solution)/shard_map/slice | solution.py:361
  32.5 0.9 fusion.3
  33.5 8.6 %halo.3.ext_ref = f32[3,34,8,128]{3,2,1,0:T(8,128)} custom-call(f32[32,8,128]{2,1,0:T(8,128)} %get-tuple-element.5.own_ref), custom_call_target="tpu_custom_call" | custom-call | tf_op jit(solution)/shard_map/halo/pallas_call | solution.py:258
  42.0 11.0 %forces.3 = (f32[32,7,128]{2,1,0:T(8,128)}, f32[32,8,128]{2,1,0:T(8,128)}) custom-call(s32[32,4]{1,0:T(8,128)} %copy.30.codes_ref, f32[3,34,8,128]{3,2,1,0:T(8,128)} %halo.3.ext_ref, f32[32,1,128]{2,1,0:T(1,128)} %slice.22.relative_ref), custom_call_target="tpu_custom_call" | custom-call | tf_op jit(solution)/shard_map/forces/pallas_call | solution.py:119
  53.0 0.9 fusion.4
  54.0 1.7 %copy.34 = f32[32,1,7,128]{3,1,2,0:T(1,128)} copy(f32[32,1,7,128]{3,2,0,1:T(8,128)} %bitcast.38) | data formatting | bytes 229376
  55.6 3.1 %copy.44 = bf16[32,1,3,126,128]{4,3,2,0,1:T(8,128)(2,1)S(1)} copy(bf16[32,1,3,126,128]{4,0,3,2,1:T(8,128)(2,1)} %param.8) | data formatting | bytes 6193152 | tf_op args[3]
  58.7 1.6 %fusion.2.gram_ref = f32[128,128]{1,0:T(8,128)} fusion(bf16[32,3,1,128]{3,2,1,0:T(2,128)(2,1)S(1)} %copy.33, bf16[32,3,1,128]{3,2,1,0:T(2,128)(2,1)S(1)} %copy.32, bf16[32,3,126,128]{3,2,1,0:T(8,128)(2,1)S(1)} %bitcast.34), kind=kOutput, calls=%fused_computation.4 | convolution fusion | flops 412090368 | bytes 3211264 | tf_op jit(solution)/shard_map/acsp,actp->st/dot_general | solution.py:364
  60.3 29.9 %reduce.1.gram_ref = f32[128,128]{1,0:T(8,128)} custom-call(f32[128,128]{1,0:T(8,128)} %fusion.2.gram_ref), custom_call_target="tpu_custom_call" | custom-call | tf_op jit(solution)/shard_map/reduce/pallas_call | solution.py:336
  90.2 26.4 %pod.1 = f32[8,128]{1,0:T(8,128)} custom-call(f32[128,128]{1,0:T(8,128)} %reduce.1.gram_ref, f32[64,128]{1,0:T(8,128)} %bitcast.42), custom_call_target="tpu_custom_call" | custom-call | tf_op jit(solution)/shard_map/pod/pallas_call | solution.py:177
  116.6 2.0 %fusion = f32[1,32,3,128]{3,0,2,1:T(1,128)S(1)} fusion(bf16[32,3,1,128]{3,2,1,0:T(2,128)(2,1)S(1)} %copy.33, bf16[32,3,1,128]{3,2,1,0:T(2,128)(2,1)S(1)} %copy.32, bf16[32,3,126,128]{3,2,1,0:T(8,128)(2,1)S(1)} %bitcast.35, f32[8,128]{1,0:T(8,128)} %pod.1), kind=kOutput, calls=%fused_computation.2 | convolution fusion | flops 28311552 | bytes 3195392 | tf_op jit(solution)/shard_map/acsp,s->acp/dot_general | solution.py:366
  118.7 0.7 copy.35
  (4 shorter events, 0.1 us)

commit v3 on v2

v3 whole, which is shorter than its diff:
```python
import functools
import math

import jax
import jax.numpy as jnp
from jax import lax
from jax.experimental import pallas as pl
from jax.experimental.pallas import tpu as pltpu
from jax.sharding import PartitionSpec as P

POD_ITERS = 4
VOLUME = 1.0 / 16.0
STIFFNESS = 100.0 / 7.0
SLOPE = -5.0 * 21.0 / (16.0 * math.pi)
DT = 0.02
SEDIMENT_EXTRA = 1.65

HI = lax.Precision.HIGHEST
NT = (((1,), (1,)), ((), ()))
NN = (((1,), (0,)), ((), ()))
TN = (((0,), (0,)), ((), ()))
BF = jnp.bfloat16
F32 = jnp.float32
MESH = pl.DeviceIdType.MESH
VM = pl.BlockSpec(memory_space=pltpu.VMEM)

TRIP = 8


def pressure_of(relative, density):
    power = relative * relative
    power = power * power * power * relative
    return STIFFNESS * (power - 1.0) / (density * relative * relative)


def prepare_kernel(state_ref, flags_ref, out_ref):
    blocks = flags_ref.shape[0]
    for field in range(6):
        out_ref[pl.ds(field, blocks, stride=8)] = state_ref[pl.ds(field, blocks, stride=7)]
    density = 1.0 + SEDIMENT_EXTRA * flags_ref[...].astype(F32)
    out_ref[pl.ds(6, blocks, stride=8)] = density * VOLUME
    out_ref[pl.ds(7, blocks, stride=8)] = pressure_of(state_ref[pl.ds(6, blocks, stride=7)], density)


def prepare(state, flags):
    blocks, part = flags.shape
    return pl.pallas_call(
        prepare_kernel,
        out_shape=jax.ShapeDtypeStruct((8 * blocks, part), F32),
        in_specs=[VM, VM],
        out_specs=VM,
        name="prepare",
    )(state, flags).reshape(blocks, 8, part)


def split3(x):
    a = x.astype(BF).astype(F32)
    b = (x - a).astype(BF).astype(F32)
    return a, b, x - a - b


def forces_kernel(codes_ref, ext_ref, state_ref, out_ref, speed_ref, *next_ref):
    blocks, part = ext_ref.shape[1] - 2, ext_ref.shape[3]
    row = lax.broadcasted_iota(jnp.int32, (8, part), 0)

    def centred(vert, stream, ds, dv):
        field = ext_ref[vert, stream]
        shift = jnp.where(row == 0, 2.0 * ds - 1.0, jnp.where(row == 1, -1.0, jnp.where(row == 2, 2.0 * dv - 1.0, 0.0)))
        return field + shift

    def norm(half):
        square = half * half
        return square[0:1] + square[1:2] + square[2:3]

    def one_block(b):
        own = centred(1, b + 1, 0.0, 0.0)
        half = 0.5 * own
        target = jnp.where(row < 3, half, jnp.where(row == 3, 1.0, jnp.where(row == 4, norm(half), 0.0)))
        h, m, l = split3(target)
        target = jnp.concatenate([h, h, m, h, l, m], axis=0).astype(BF)
        lefts, rights = [], []
        for n in range(5):
            if n == 0:
                vert, stream, ds, dv = 1, b + 1, 0.0, 0.0
            else:
                code = codes_ref[n - 1, b]
                code = jnp.where(code >= 4, code + 1, code)
                third = lax.div(code, 3)
                ds, dv = third - 1, code - 3 * third - 1
                vert, stream = dv + 1, b + 1 + ds
                ds, dv = ds.astype(F32), dv.astype(F32)
            near = centred(vert, stream, ds, dv)
            half = 0.5 * near
            source = jnp.where(row < 3, -2.0 * half, jnp.where(row == 3, norm(half), jnp.where(row == 4, 1.0, 0.0)))
            h, m, l = split3(source)
            source = jnp.concatenate([h, m, h, l, h, m], axis=0).astype(BF)
            mass = near[6:7]
            weighted = jnp.where(row == 6, 1.0, near) * mass
            dots = near[0:3] * near[3:6]
            dot = mass * (dots[0:1] + dots[1:2] + dots[2:3])
            second = jnp.where(row < 3, weighted * near[7:8], jnp.where(row == 3, dot, 0.0))
            fields = jnp.concatenate([weighted, second], axis=0)
            high = fields.astype(BF)
            low = (fields - high.astype(F32)).astype(BF)
            quarter = lax.dot_general(target, source, TN, preferred_element_type=F32)
            quarter = jnp.maximum(quarter, 1e-30)
            reach = jnp.maximum(1.0 - quarter * lax.rsqrt(quarter), 0.0)
            cube = reach * reach * reach
            cube_high = cube.astype(BF)
            cube_low = (cube - cube_high.astype(F32)).astype(BF)
            left = jnp.concatenate([cube_high, cube_low], axis=1)
            right = jnp.concatenate([jnp.concatenate([high, high], axis=1), jnp.concatenate([low, jnp.zeros_like(low)], axis=1)], axis=0)
            lefts.append(left)
            rights.append(right)
        sums = lax.dot_general(jnp.concatenate(lefts, axis=1), jnp.concatenate(rights, axis=1), NT, preferred_element_type=F32)
        sums = jnp.transpose(sums)
        sums = sums[0:16] + sums[16:32]
        relative = state_ref[pl.ds(7 * b + 6, 1)]
        density = 16.0 * own[6:7]
        place, speed, pressure = own[0:3], own[3:6], own[7:8]
        total, pressure_total, vx = sums[6:7], sums[7:8], sums[11:12]
        dots = speed * (place * total - sums[0:3]) - place * sums[3:6]
        rate = SLOPE * (dots[0:1] + dots[1:2] + dots[2:3] + vx)
        acc = -SLOPE * (pressure * (place * total - sums[0:3]) + place * pressure_total - sums[8:11])
        gravity = jnp.where(row[0:3] == 2, -1.0, 0.0)
        speed = speed + DT * (acc + gravity)
        place = ext_ref[1, b + 1][0:3] + DT * speed
        relative = relative + DT * rate / density
        out_ref[pl.ds(7 * b, 7)] = jnp.concatenate([place, speed, relative], axis=0)
        for c in range(3):
            speed_ref[c, pl.ds(b, 1)] = speed[c : c + 1]
        if next_ref:
            pressure = pressure_of(relative, density)
            next_ref[0][b] = jnp.concatenate([place, speed, own[6:7], pressure], axis=0)

    def several(i, carry):
        for k in range(TRIP):
            one_block(TRIP * i + k)
        return carry

    lax.fori_loop(0, blocks // TRIP, several, 0)


def forces_step(codes, ext, state, last):
    blocks, part = ext.shape[1] - 2, ext.shape[3]
    shapes = [jax.ShapeDtypeStruct(state.shape, F32), jax.ShapeDtypeStruct((3, blocks, part), F32)]
    if not last:
        shapes.append(jax.ShapeDtypeStruct((blocks, 8, part), F32))
    return pl.pallas_call(
        forces_kernel,
        out_shape=shapes,
        in_specs=[pl.BlockSpec(memory_space=pltpu.SMEM), VM, VM],
        out_specs=[VM] * len(shapes),
        name="forces",
    )(codes, ext, state)


def orthonormal_rows(t):
    rank, width = t.shape
    zero = jnp.zeros((width - rank, width), jnp.float32)
    lane = lax.broadcasted_iota(jnp.int32, (rank, width), 1)
    row = lax.broadcasted_iota(jnp.int32, (rank, width), 0)
    unit = jnp.where(lane == row + rank, 1.0, 0.0)
    work = lax.dot_general(t, jnp.concatenate([t, zero], axis=0), NT, precision=HI) + unit
    eight = lax.broadcasted_iota(jnp.int32, (8, width), 0)
    count = rank // 8

    groups = [work[8 * g:8 * g + 8] for g in range(count)]
    for p in range(count):
        live = range(p, count)
        cols = [{g: jnp.broadcast_to(groups[g][:, 8 * p + c:8 * p + c + 1], (8, width)) for g in live} for c in range(8)]
        for k in range(8):
            inv = lax.rsqrt(jnp.broadcast_to(cols[k][p][k:k + 1], (8, width)))
            low = {g: cols[k][g] * inv for g in live}
            pivot_row = jnp.broadcast_to(groups[p][k:k + 1], (8, width)) * inv
            for c in range(k + 1, 8):
                factor = jnp.broadcast_to(low[p][c:c + 1], (8, width))
                for g in live:
                    cols[c][g] = cols[c][g] - low[g] * factor
            groups[p] = jnp.where(eight == k, pivot_row, jnp.where(eight > k, groups[p] - low[p] * pivot_row, groups[p]))
            for g in range(p + 1, count):
                groups[g] = groups[g] - low[g] * pivot_row
    done = jnp.concatenate(groups, axis=0)
    return lax.dot_general(done, jnp.concatenate([zero, t], axis=0), NN, precision=HI)
def pod_kernel(iters, gram_ref, rows_ref, basis_ref, out_ref, full_ref):
    width = gram_ref.shape[0]
    rows = rows_ref[...]
    across = jnp.transpose(jnp.concatenate([rows, jnp.zeros((width - rows.shape[0], width), F32)], axis=0))
    lane = lax.broadcasted_iota(jnp.int32, (width, width), 1)
    row = lax.broadcasted_iota(jnp.int32, (width, width), 0)
    full = gram_ref[...]
    for k in range(2):
        place = width - 2 + k
        full = jnp.where(lane == place, jnp.broadcast_to(across[:, k : k + 1], full.shape), full)
        full = jnp.where(row == place, jnp.broadcast_to(rows[k : k + 1], full.shape), full)
    full_ref[...] = full

    def times_gram(t):
        return lax.dot_general(t, full_ref[...], NN, precision=HI)

    def half(i, t):
        t = orthonormal_rows(t)
        again = jnp.logical_and(i % 2 == 1, i < 2 * iters - 1)
        return lax.cond(again, times_gram, lambda t: t, t)

    t = lax.fori_loop(0, 2 * iters, half, times_gram(basis_ref[...]))
    last = jnp.broadcast_to(t[:, width - 1 : width], t.shape)
    out_ref[...] = jnp.broadcast_to(jnp.sum(t * last, axis=0, keepdims=True), out_ref.shape)


def pod_weights(gram, rows, basis):
    return pl.pallas_call(
        functools.partial(pod_kernel, POD_ITERS),
        out_shape=jax.ShapeDtypeStruct((8, gram.shape[0]), F32),
        in_specs=[VM] * 3,
        out_specs=VM,
        scratch_shapes=[pltpu.VMEM(gram.shape, F32)],
        name="pod",
    )(gram, rows, basis)


SIDES = [(ds, dv) for dv in (-1, 0, 1) for ds in (-1, 0, 1) if (ds, dv) != (0, 0)]
LONG = 8


def present(ds, dv):
    s, v = lax.axis_index("stream") + ds, lax.axis_index("vert") + dv
    inside_s = jnp.logical_and(s >= 0, s < lax.axis_size("stream"))
    return jnp.logical_and(inside_s, jnp.logical_and(v >= 0, v < lax.axis_size("vert")))


def halo_copy(own_ref, ext_ref, send_sem, recv_sem, index):
    blocks = own_ref.shape[0]
    ds, dv = SIDES[index]
    if ds == 0:
        source, target = own_ref, ext_ref.at[1 - dv, pl.ds(1, blocks)]
    elif ds == 1:
        source, target = own_ref.at[pl.ds(blocks - 1, 1)], ext_ref.at[1 - dv, pl.ds(0, 1)]
    else:
        source, target = own_ref.at[pl.ds(0, 1)], ext_ref.at[1 - dv, pl.ds(blocks + 1, 1)]
    return pltpu.make_async_remote_copy(
        src_ref=source,
        dst_ref=target,
        send_sem=send_sem.at[index],
        recv_sem=recv_sem.at[index],
        device_id=(lax.axis_index("stream") + ds, lax.axis_index("vert") + dv),
        device_id_type=MESH,
    )


def halo_greet(barrier):
    count = 0
    for ds, dv in SIDES:
        here = present(ds, dv)
        count = count + here.astype(jnp.int32)

        @pl.when(here)
        def _():
            device = (lax.axis_index("stream") + ds, lax.axis_index("vert") + dv)
            pl.semaphore_signal(barrier, inc=1, device_id=device, device_id_type=MESH)

    return count


def halo_start(own_ref, ext_ref, send_sem, recv_sem):
    blocks = own_ref.shape[0]
    for index in (1, 6, 0, 2, 3, 4, 5, 7):
        ds, dv = SIDES[index]

        @pl.when(present(ds, dv))
        def _():
            halo_copy(own_ref, ext_ref, send_sem, recv_sem, index).start()

        @pl.when(jnp.logical_not(present(ds, dv)))
        def _():
            if ds == 0:
                ext_ref[1 + dv, 1 : blocks + 1] = jnp.zeros(own_ref.shape, F32)
            else:
                ext_ref[1 + dv, 0 if ds < 0 else blocks + 1] = jnp.zeros(own_ref.shape[1:], F32)


def halo_finish(own_ref, ext_ref, send_sem, recv_sem):
    for index, (ds, dv) in enumerate(SIDES):
        back = SIDES.index((-ds, -dv))

        @pl.when(present(ds, dv))
        def _():
            halo_copy(own_ref, ext_ref, send_sem, recv_sem, index).wait_send()
            halo_copy(own_ref, ext_ref, send_sem, recv_sem, back).wait_recv()


def groups():
    stream, vert = lax.axis_index("stream"), lax.axis_index("vert")
    core, z, y = stream % 2, (stream // 2) % LONG, stream // (2 * LONG)
    return (
        (vert * 2 + core, lambda r: (stream - core + r % 2, r // 2)),
        (z, lambda r: (stream + (r - z) * 2, vert)),
        (y, lambda r: (stream + (r - y) * 2 * LONG, vert)),
    )


def group_greet(barrier, me, device):
    for step in range(1, LONG):
        pl.semaphore_signal(barrier, inc=1, device_id=device((me + step) % LONG), device_id_type=MESH)
    return LONG - 1


def group_copies(me, device, source, target, send_sem, recv_sem):
    copies = []
    for step in range(1, LONG):
        other = (me + step) % LONG
        copies.append(
            pltpu.make_async_remote_copy(
                src_ref=source(other),
                dst_ref=target(step),
                send_sem=send_sem.at[step],
                recv_sem=recv_sem.at[step],
                device_id=device(other),
                device_id_type=MESH,
            )
        )
    return copies


def start(copies):
    for copy in copies:
        copy.start()


def finish(copies):
    for copy in copies:
        copy.wait()


def total(own, slots_ref):
    for step in range(1, LONG):
        own = own + slots_ref[step]
    return own


def shard_of(index, size):
    return pl.ds(pl.multiple_of(index * size, size), size)


def first_kernel(own_ref, gram_ref, start_ref, ext_ref, part_ref, basis_ref, slots, local_sem, send, recv, gsend, grecv):
    near = groups()[0]
    size = gram_ref.shape[0] // LONG
    local = pltpu.make_async_copy(own_ref, ext_ref.at[1, pl.ds(1, own_ref.shape[0])], local_sem)
    local.start()
    barrier = pltpu.get_barrier_semaphore()
    pl.semaphore_wait(barrier, halo_greet(barrier) + group_greet(barrier, *near))
    halo_start(own_ref, ext_ref, send, recv)
    copies = group_copies(*near, lambda other: gram_ref.at[shard_of(other, size)], lambda step: slots.at[step], gsend, grecv)
    start(copies)
    basis_ref[...] = start_ref[...]

    @pl.loop(0, 2)
    def _(i):
        basis_ref[...] = orthonormal_rows(basis_ref[...])

    finish(copies)
    part_ref[...] = total(gram_ref[shard_of(near[0], size)], slots)
    halo_finish(own_ref, ext_ref, send, recv)
    local.wait()


def second_kernel(own_ref, part_ref, ext_ref, out_ref, slots, sums, local_sem, send, recv, gsend, grecv):
    _, z, y = groups()
    local = pltpu.make_async_copy(own_ref, ext_ref.at[1, pl.ds(1, own_ref.shape[0])], local_sem)
    local.start()
    barrier = pltpu.get_barrier_semaphore()
    pl.semaphore_wait(barrier, halo_greet(barrier) + group_greet(barrier, *z) + group_greet(barrier, *y))
    copies = group_copies(*z, lambda other: part_ref, lambda step: slots.at[0, step], gsend.at[0], grecv.at[0])
    start(copies)
    halo_start(own_ref, ext_ref, send, recv)
    finish(copies)
    sums[...] = total(part_ref[...], slots.at[0])
    copies = group_copies(*y, lambda other: sums, lambda step: slots.at[1, step], gsend.at[1], grecv.at[1])
    start(copies)
    halo_finish(own_ref, ext_ref, send, recv)
    finish(copies)
    out_ref[...] = total(sums[...], slots.at[1])
    local.wait()


def third_kernel(rows_ref, part_ref, rows_out, gram_out, slots, sums, send, recv, gsend, grecv, local_sem):
    near, z, y = groups()
    size = part_ref.shape[0]
    barrier = pltpu.get_barrier_semaphore()
    local = pltpu.make_async_copy(part_ref, gram_out.at[shard_of(near[0], size)], local_sem)
    local.start()
    pl.semaphore_wait(barrier, group_greet(barrier, *near) + group_greet(barrier, *z) + group_greet(barrier, *y))
    gathers = group_copies(*near, lambda other: part_ref, lambda step: gram_out.at[shard_of(near[0], size)], gsend, grecv)
    source, value = rows_ref, rows_ref[...]
    for stage, group in enumerate((z, y, near)):
        copies = group_copies(
            *group, lambda other: source, lambda step: slots.at[stage, step], send.at[stage], recv.at[stage]
        )
        start(copies)
        if stage == 0:
            start(gathers)
        finish(copies)
        value = total(value, slots.at[stage])
        if stage < 2:
            sums[stage] = value
            source = sums.at[stage]
    rows_out[...] = value
    finish(gathers)
    local.wait()


def remote(kernel, name, collective_id, operands, shapes, scratch):
    return pl.pallas_call(
        kernel,
        out_shape=[jax.ShapeDtypeStruct(shape, F32) for shape in shapes],
        in_specs=[VM] * len(operands),
        out_specs=[VM] * len(shapes),
        scratch_shapes=scratch,
        compiler_params=pltpu.CompilerParams(collective_id=collective_id, has_side_effects=True),
        name=name,
    )(*operands)


def body(particles, phase_flags, neighbours, history, basis_start):
    blocks, _, fields, part = particles.shape
    snaps, rank = basis_start.shape
    state = particles.reshape(blocks * fields, part)
    codes = neighbours[:, 0].T
    past = jnp.transpose(history[:, 0], (1, 2, 0, 3))
    dma = pltpu.SemaphoreType.DMA
    payload = prepare(state, phase_flags[:, 0])
    gram = jnp.einsum("csbp,ctbp->st", past, past, preferred_element_type=F32)
    gram = jnp.pad(gram, ((0, 2), (0, 2)))
    wide = (3, blocks + 2, 8, part)
    shard = snaps // LONG
    ext, piece, basis = remote(
        first_kernel, "first", 0, (payload, gram, basis_start.T), (wide, (shard, snaps), (rank, snaps)),
        [pltpu.VMEM((LONG, shard, snaps), F32), dma, dma((8,)), dma((8,)), dma((LONG,)), dma((LONG,))],
    )
    state, speed_1, payload = forces_step(codes, ext, state, False)
    ext, piece = remote(
        second_kernel, "second", 1, (payload, piece), (wide, (shard, snaps)),
        [pltpu.VMEM((2, LONG, shard, snaps), F32), pltpu.VMEM((shard, snaps), F32), dma, dma((8,)), dma((8,)),
         dma((2, LONG)), dma((2, LONG))],
    )
    state, speed_2 = forces_step(codes, ext, state, True)
    newest = jnp.stack([speed_1, speed_2]).astype(BF)
    with_past = jnp.einsum("kcbp,csbp->ks", newest, past, preferred_element_type=F32)
    with_newest = jnp.einsum("kcbp,lcbp->kl", newest, newest, preferred_element_type=F32)
    rows = jnp.pad(jnp.concatenate([with_past, with_newest], axis=1), ((0, 6), (0, 0)))
    rows, gram = remote(
        third_kernel, "third", 2, (rows, piece), ((8, snaps), (snaps, snaps)),
        [pltpu.VMEM((3, LONG, 8, snaps), F32), pltpu.VMEM((2, 8, snaps), F32), dma((3, LONG)), dma((3, LONG)),
         dma((LONG,)), dma((LONG,)), dma],
    )
    weights = pod_weights(gram, rows, basis)[0]
    filtered = jnp.sum(past.astype(F32) * weights[:-2, None, None], axis=1)
    for k in range(2):
        filtered = filtered + weights[snaps - 2 + k] * newest[k].astype(F32)
    filtered = jnp.transpose(filtered, (1, 0, 2))
    return (state.reshape(particles.shape), filtered[:, None])


def solution(mesh):
    in_specs = (
        P("stream", "vert", None, None),
        P("stream", "vert", None),
        P("stream", "vert", None),
        P("stream", "vert", None, None, None),
        P(),
    )
    out_specs = (P("stream", "vert", None, None), P("stream", "vert", None, None))
    return jax.shard_map(body, mesh=mesh, in_specs=in_specs, out_specs=out_specs, check_vma=False)
```

time: 120 us -> 114 us (0.950)
  local copies, waits for them, and re-layouts: 11.2 us -> 3.43 us
  matrix products: 3.63 us -> 8.34 us
  Pallas kernels: 102 us -> 97.4 us
  other arithmetic: 2.1 us -> 3.44 us
    unnamed x3, local copies, waits for them, and re-layouts: 5.42 us -> 0.68 us
    dot_general x2 -> x3, matrix products: 3.63 us -> 8.34 us  [the longest x1 6.26 us: body(): gram = jnp.einsum('csbp,ctbp->st', past, past, preferred_element_type=F32)]
    pallas_call x6 -> x7, Pallas kernels: 102 us -> 97.4 us  [the longest x3 57.7 us: remote(): pl.pallas_call(kernel, out_shape=[jax.ShapeDtypeStruct(shape, F32) for sh...]
    squeeze x2 -> x0, local copies, waits for them, and re-layouts: 2.27 us -> none  [the longest x1 1.37 us: body(): codes = neighbours[:, 0]]
    another operation x4 -> x0, local copies, waits for them, and re-layouts: 1.93 us -> none  [body(): newest = jnp.stack([first[:, 3:6], second[:, 3:6]], axis=2).astype(BF)]
    broadcast_in_dim x0 -> x1, other arithmetic: none -> 1.26 us  [body(): return (state.reshape(particles.shape), filtered[:, None])]
where the time goes in v3:
time: 114 us; the launch traced here: 113 us
  Pallas kernels  97.4 us (85%)
  matrix products  8.34 us (7%)
  other arithmetic  3.44 us (3%)
  local copies, waits for them, and re-layouts  3.43 us (3%)
    pallas_call x3, Pallas kernels, remote(): pl.pallas_call(kernel, out_shape=[jax.ShapeDtypeStruct(shape, F32) for sh...  57.7 us
    pallas_call x1, Pallas kernels, pod_weights(): pl.pallas_call(functools.partial(pod_kernel, POD_ITERS), out_shape=jax.Sh...  19.4 us
    pallas_call x2, Pallas kernels, forces_step(): pl.pallas_call(forces_kernel, out_shape=shapes, in_specs=[pl.BlockSpec(me...  18.7 us
    dot_general x1, matrix products, body(): gram = jnp.einsum('csbp,ctbp->st', past, past, preferred_element_type=F32)  6.26 us

profile of v3, /device:TPU:1, one launch (start us, length us, event | category | flops | bytes accessed | tf_op | source)
XLA Modules:
  0.0 113.3 jit_solution(11543785687925698673)
XLA Ops:
  0.6 0.0 copy-start
  0.6 6.3 %fusion.4 = f32[126,126]{1,0:T(8,128)S(1)} fusion(bf16[3,126,32,128]{3,2,1,0:T(8,128)(2,1)} %bitcast.44), kind=kOutput, calls=%fused_computation.5 | convolution fusion | flops 390168576 | bytes 3160080 | tf_op jit(solution)/shard_map/csbp,ctbp->st/dot_general | solution.py:432
  6.9 0.6 pad.8.gram_ref
  7.6 1.6 %prepare.1 = f32[256,128]{1,0:T(8,128)} custom-call(f32[224,128]{1,0:T(8,128)} %bitcast.47, s32[32,128]{1,0:T(8,128)} %bitcast.50), custom_call_target="tpu_custom_call" | custom-call | tf_op jit(solution)/shard_map/prepare/pallas_call | solution.py:47
  9.1 17.5 %first.1 = (f32[3,34,8,128]{3,2,1,0:T(8,128)}, f32[16,128]{1,0:T(8,128)}, f32[64,128]{1,0:T(8,128)}) custom-call(f32[32,8,128]{2,1,0:T(8,128)} %bitcast.46, f32[128,128]{1,0:T(8,128)} %pad.8.gram_ref, f32[64,128]{1,0:T(8,128)} %bitcast.49), custom_call_target="tpu_custom_call" | custom-call | tf_op jit(solution)/shard_map/first/pallas_call | solution.py:413
  26.6 9.4 %forces.2 = (f32[224,128]{1,0:T(8,128)}, f32[3,32,128]{2,1,0:T(8,128)}, f32[32,8,128]{2,1,0:T(8,128)}) custom-call(s32[4,32]{1,0:T(4,128)} %bitcast.51, f32[3,34,8,128]{3,2,1,0:T(8,128)} %get-tuple-element.14.ext_ref, f32[224,128]{1,0:T(8,128)} %bitcast.48), custom_call_target="tpu_custom_call" | custom-call | tf_op jit(solution)/shard_map/forces/pallas_call | solution.py:149
  36.0 18.9 %second.1 = (f32[3,34,8,128]{3,2,1,0:T(8,128)}, f32[16,128]{1,0:T(8,128)}) custom-call(f32[32,8,128]{2,1,0:T(8,128)} %get-tuple-element.15.own_ref, f32[16,128]{1,0:T(8,128)} %get-tuple-element.16.part_ref), custom_call_target="tpu_custom_call" | custom-call | tf_op jit(solution)/shard_map/second/pallas_call | solution.py:413
  54.9 9.3 %forces.3 = (f32[224,128]{1,0:T(8,128)}, f32[3,32,128]{2,1,0:T(8,128)}) custom-call(s32[4,32]{1,0:T(4,128)} %bitcast.52, f32[3,34,8,128]{3,2,1,0:T(8,128)} %get-tuple-element.17.ext_ref, f32[224,128]{1,0:T(8,128)} %get-tuple-element.18.state_ref), custom_call_target="tpu_custom_call" | custom-call | tf_op jit(solution)/shard_map/forces/pallas_call | solution.py:149
  64.2 0.8 convert_bitcast_fusion
  65.0 0.2 convolution_bitcast_fusion
  65.3 0.0 copy-done
  65.3 1.8 %fusion.7 = f32[2,126]{1,0:T(2,128)S(1)} fusion(bf16[3,126,32,128]{3,2,1,0:T(8,128)(2,1)S(1)} %bitcast.45, bf16[2,3,32,128]{3,2,1,0:T(8,128)(2,1)S(1)} %pad_maximum_fusion), kind=kOutput, calls=%fused_computation.6 | convolution fusion | flops 6193152 | bytes 3146736 | tf_op jit(solution)/shard_map/kcbp,csbp->ks/dot_general | solution.py:448
  67.1 0.7 select_maximum_fusion.rows_ref
  67.8 21.3 %third.1 = (f32[8,128]{1,0:T(8,128)}, f32[128,128]{1,0:T(8,128)}) custom-call(f32[8,128]{1,0:T(8,128)} %select_maximum_fusion.rows_ref, f32[16,128]{1,0:T(8,128)} %get-tuple-element.22.part_ref), custom_call_target="tpu_custom_call" | custom-call | tf_op jit(solution)/shard_map/third/pallas_call | solution.py:413
  89.2 19.4 %pod.1 = f32[8,128]{1,0:T(8,128)} custom-call(f32[128,128]{1,0:T(8,128)} %get-tuple-element.23.gram_ref, f32[8,128]{1,0:T(8,128)} %get-tuple-element.24.rows_ref, f32[64,128]{1,0:T(8,128)} %get-tuple-element.25.basis_ref), custom_call_target="tpu_custom_call" | custom-call | tf_op jit(solution)/shard_map/pod/pallas_call | solution.py:212
  108.6 0.7 slice_bitcast_fusion
  109.2 1.4 %fusion.13 = (f32[1,1]{1,0:T(1,128)}, f32[1,1]{1,0:T(1,128)}) fusion(f32[8,128]{1,0:T(8,128)} %pod.1), kind=kLoop, calls=%fused_computation.19 | loop fusion | bytes 16 | tf_op jit(solution)/shard_map/slice | solution.py:459
  110.7 0.7 multiply_reduce_fusion
  111.3 1.3 %fusion.10 = f32[32,1,3,128]{3,0,2,1:T(8,128)S(1)} fusion(f32[3,32,128]{2,1,0:T(8,128)S(1)} %multiply_reduce_fusion, bf16[1,3,32,128]{3,2,1,0:T(8,128)(2,1)S(1)} %get-tuple-element.32, bf16[1,3,32,128]{3,2,1,0:T(8,128)(2,1)S(1)} %get-tuple-element.33, f32[]{:T(128)} %bitcast.22, f32[]{:T(128)} %bitcast.20), kind=kLoop, calls=%fused_computation.10 | loop fusion | flops 73728 | bytes 147464 | tf_op jit(solution)/shard_map/broadcast_in_dim | solution.py:461
  112.6 0.7 copy.22
  (1 shorter events, 0.0 us)
Async XLA Ops:
  0.6 64.7 %copy-start = (bf16[32,1,3,126,128]{4,0,3,2,1:T(8,128)(2,1)S(1)}, bf16[32,1,3,126,128]{4,0,3,2,1:T(8,128)(2,1)}, u32[]{:S(2)}) copy-start(bf16[32,1,3,126,128]{4,0,3,2,1:T(8,128)(2,1)} %param.8) | copy-start | bytes 9289732

commit v4 on v3

v4 whole, which is shorter than its diff:
```python
import functools
import math

import jax
import jax.numpy as jnp
from jax import lax
from jax.experimental import pallas as pl
from jax.experimental.pallas import tpu as pltpu
from jax.sharding import PartitionSpec as P

POD_ITERS = 4
VOLUME = 1.0 / 16.0
STIFFNESS = 100.0 / 7.0
SLOPE = -5.0 * 21.0 / (16.0 * math.pi)
DT = 0.02
SEDIMENT_EXTRA = 1.65

HI = lax.Precision.HIGHEST
NT = (((1,), (1,)), ((), ()))
NN = (((1,), (0,)), ((), ()))
TN = (((0,), (0,)), ((), ()))
BF = jnp.bfloat16
F32 = jnp.float32
MESH = pl.DeviceIdType.MESH
VM = pl.BlockSpec(memory_space=pltpu.VMEM)

TRIP = 8


def pressure_of(relative, density):
    power = relative * relative
    power = power * power * power * relative
    return STIFFNESS * (power - 1.0) / (density * relative * relative)


def split3(x):
    a = x.astype(BF).astype(F32)
    b = (x - a).astype(BF).astype(F32)
    return a, b, x - a - b


def forces(codes_ref, ext_ref, state_ref, out_ref, speed_ref, next_ref=None):
    blocks, part = ext_ref.shape[1] - 2, ext_ref.shape[3]
    row = lax.broadcasted_iota(jnp.int32, (8, part), 0)

    def centred(vert, stream, ds, dv):
        field = ext_ref[vert, stream]
        shift = jnp.where(row == 0, 2.0 * ds - 1.0, jnp.where(row == 1, -1.0, jnp.where(row == 2, 2.0 * dv - 1.0, 0.0)))
        return field + shift

    def norm(half):
        square = half * half
        return square[0:1] + square[1:2] + square[2:3]

    def one_block(b):
        own = centred(1, b + 1, 0.0, 0.0)
        half = 0.5 * own
        target = jnp.where(row < 3, half, jnp.where(row == 3, 1.0, jnp.where(row == 4, norm(half), 0.0)))
        h, m, l = split3(target)
        target = jnp.concatenate([h, h, m, h, l, m], axis=0).astype(BF)
        lefts, rights = [], []
        for n in range(5):
            if n == 0:
                vert, stream, ds, dv = 1, b + 1, 0.0, 0.0
            else:
                code = codes_ref[n - 1, b]
                code = jnp.where(code >= 4, code + 1, code)
                third = lax.div(code, 3)
                ds, dv = third - 1, code - 3 * third - 1
                vert, stream = dv + 1, b + 1 + ds
                ds, dv = ds.astype(F32), dv.astype(F32)
            near = centred(vert, stream, ds, dv)
            half = 0.5 * near
            source = jnp.where(row < 3, -2.0 * half, jnp.where(row == 3, norm(half), jnp.where(row == 4, 1.0, 0.0)))
            h, m, l = split3(source)
            source = jnp.concatenate([h, m, h, l, h, m], axis=0).astype(BF)
            mass = near[6:7]
            weighted = jnp.where(row == 6, 1.0, near) * mass
            dots = near[0:3] * near[3:6]
            dot = mass * (dots[0:1] + dots[1:2] + dots[2:3])
            second = jnp.where(row < 3, weighted * near[7:8], jnp.where(row == 3, dot, 0.0))
            fields = jnp.concatenate([weighted, second], axis=0)
            high = fields.astype(BF)
            low = (fields - high.astype(F32)).astype(BF)
            quarter = lax.dot_general(target, source, TN, preferred_element_type=F32)
            quarter = jnp.maximum(quarter, 1e-30)
            reach = jnp.maximum(1.0 - quarter * lax.rsqrt(quarter), 0.0)
            cube = reach * reach * reach
            cube_high = cube.astype(BF)
            cube_low = (cube - cube_high.astype(F32)).astype(BF)
            left = jnp.concatenate([cube_high, cube_low], axis=1)
            right = jnp.concatenate([jnp.concatenate([high, high], axis=1), jnp.concatenate([low, jnp.zeros_like(low)], axis=1)], axis=0)
            lefts.append(left)
            rights.append(right)
        sums = lax.dot_general(jnp.concatenate(lefts, axis=1), jnp.concatenate(rights, axis=1), NT, preferred_element_type=F32)
        sums = jnp.transpose(sums)
        sums = sums[0:16] + sums[16:32]
        relative = state_ref[pl.ds(7 * b + 6, 1)]
        density = 16.0 * own[6:7]
        place, speed, pressure = own[0:3], own[3:6], own[7:8]
        total, pressure_total, vx = sums[6:7], sums[7:8], sums[11:12]
        dots = speed * (place * total - sums[0:3]) - place * sums[3:6]
        rate = SLOPE * (dots[0:1] + dots[1:2] + dots[2:3] + vx)
        acc = -SLOPE * (pressure * (place * total - sums[0:3]) + place * pressure_total - sums[8:11])
        gravity = jnp.where(row[0:3] == 2, -1.0, 0.0)
        speed = speed + DT * (acc + gravity)
        place = ext_ref[1, b + 1][0:3] + DT * speed
        relative = relative + DT * rate / density
        out_ref[pl.ds(7 * b, 7)] = jnp.concatenate([place, speed, relative], axis=0)
        for c in range(3):
            speed_ref[c, pl.ds(b, 1)] = speed[c : c + 1]
        if next_ref is not None:
            pressure = pressure_of(relative, density)
            next_ref[1, b + 1] = jnp.concatenate([place, speed, own[6:7], pressure], axis=0)

    def several(i, carry):
        for k in range(TRIP):
            one_block(TRIP * i + k)
        return carry

    lax.fori_loop(0, blocks // TRIP, several, 0)


def orthonormal_rows(t):
    rank, width = t.shape
    zero = jnp.zeros((width - rank, width), jnp.float32)
    lane = lax.broadcasted_iota(jnp.int32, (rank, width), 1)
    row = lax.broadcasted_iota(jnp.int32, (rank, width), 0)
    unit = jnp.where(lane == row + rank, 1.0, 0.0)
    work = lax.dot_general(t, jnp.concatenate([t, zero], axis=0), NT, precision=HI) + unit
    eight = lax.broadcasted_iota(jnp.int32, (8, width), 0)
    count = rank // 8

    groups = [work[8 * g:8 * g + 8] for g in range(count)]
    for p in range(count):
        live = range(p, count)
        cols = [{g: jnp.broadcast_to(groups[g][:, 8 * p + c:8 * p + c + 1], (8, width)) for g in live} for c in range(8)]
        for k in range(8):
            inv = lax.rsqrt(jnp.broadcast_to(cols[k][p][k:k + 1], (8, width)))
            low = {g: cols[k][g] * inv for g in live}
            pivot_row = jnp.broadcast_to(groups[p][k:k + 1], (8, width)) * inv
            for c in range(k + 1, 8):
                factor = jnp.broadcast_to(low[p][c:c + 1], (8, width))
                for g in live:
                    cols[c][g] = cols[c][g] - low[g] * factor
            groups[p] = jnp.where(eight == k, pivot_row, jnp.where(eight > k, groups[p] - low[p] * pivot_row, groups[p]))
            for g in range(p + 1, count):
                groups[g] = groups[g] - low[g] * pivot_row
    done = jnp.concatenate(groups, axis=0)
    return lax.dot_general(done, jnp.concatenate([zero, t], axis=0), NN, precision=HI)
SIDES = [(ds, dv) for dv in (-1, 0, 1) for ds in (-1, 0, 1) if (ds, dv) != (0, 0)]
LONG = 8


def present(ds, dv):
    s, v = lax.axis_index("stream") + ds, lax.axis_index("vert") + dv
    inside_s = jnp.logical_and(s >= 0, s < lax.axis_size("stream"))
    return jnp.logical_and(inside_s, jnp.logical_and(v >= 0, v < lax.axis_size("vert")))


def halo_copy(ext_ref, send_sem, recv_sem, index):
    blocks = ext_ref.shape[1] - 2
    ds, dv = SIDES[index]
    if ds == 0:
        source, target = pl.ds(1, blocks), pl.ds(1, blocks)
    elif ds == 1:
        source, target = pl.ds(blocks, 1), pl.ds(0, 1)
    else:
        source, target = pl.ds(1, 1), pl.ds(blocks + 1, 1)
    source, target = ext_ref.at[1, source], ext_ref.at[1 - dv, target]
    return pltpu.make_async_remote_copy(
        src_ref=source,
        dst_ref=target,
        send_sem=send_sem.at[index],
        recv_sem=recv_sem.at[index],
        device_id=(lax.axis_index("stream") + ds, lax.axis_index("vert") + dv),
        device_id_type=MESH,
    )


def halo_greet(barrier):
    count = 0
    for ds, dv in SIDES:
        here = present(ds, dv)
        count = count + here.astype(jnp.int32)

        @pl.when(here)
        def _():
            device = (lax.axis_index("stream") + ds, lax.axis_index("vert") + dv)
            pl.semaphore_signal(barrier, inc=1, device_id=device, device_id_type=MESH)

    return count


def halo_clear(ext_ref):
    blocks, fields, part = ext_ref.shape[1] - 2, ext_ref.shape[2], ext_ref.shape[3]
    for ds, dv in SIDES:

        @pl.when(jnp.logical_not(present(ds, dv)))
        def _():
            if ds == 0:
                ext_ref[1 + dv, 1 : blocks + 1] = jnp.zeros((blocks, fields, part), F32)
            else:
                ext_ref[1 + dv, 0 if ds < 0 else blocks + 1] = jnp.zeros((fields, part), F32)


def halo_start(ext_ref, send_sem, recv_sem):
    for index in (1, 6, 0, 2, 3, 4, 5, 7):

        @pl.when(present(*SIDES[index]))
        def _():
            halo_copy(ext_ref, send_sem, recv_sem, index).start()


def halo_finish(ext_ref, send_sem, recv_sem):
    for index, (ds, dv) in enumerate(SIDES):
        back = SIDES.index((-ds, -dv))

        @pl.when(present(ds, dv))
        def _():
            halo_copy(ext_ref, send_sem, recv_sem, index).wait_send()
            halo_copy(ext_ref, send_sem, recv_sem, back).wait_recv()


def groups():
    stream, vert = lax.axis_index("stream"), lax.axis_index("vert")
    core, z, y = stream % 2, (stream // 2) % LONG, stream // (2 * LONG)
    return (
        (vert * 2 + core, lambda r: (stream - core + r % 2, r // 2)),
        (z, lambda r: (stream + (r - z) * 2, vert)),
        (y, lambda r: (stream + (r - y) * 2 * LONG, vert)),
    )


def group_greet(barrier, me, device):
    for step in range(1, LONG):
        pl.semaphore_signal(barrier, inc=1, device_id=device((me + step) % LONG), device_id_type=MESH)
    return LONG - 1


def group_copies(me, device, source, target, send_sem, recv_sem):
    copies = []
    for step in range(1, LONG):
        other = (me + step) % LONG
        copies.append(
            pltpu.make_async_remote_copy(
                src_ref=source(other),
                dst_ref=target(step),
                send_sem=send_sem.at[step],
                recv_sem=recv_sem.at[step],
                device_id=device(other),
                device_id_type=MESH,
            )
        )
    return copies


def start(copies):
    for copy in copies:
        copy.start()


def finish(copies):
    for copy in copies:
        copy.wait()


def total(own, slots_ref):
    for step in range(1, LONG):
        own = own + slots_ref[step]
    return own


def shard_of(index, size):
    return pl.ds(pl.multiple_of(index * size, size), size)


def rounded(speed_ref):
    return [speed_ref[c].astype(BF).astype(F32) for c in range(3)]


def plane_products(planes, others, products_ref, s):
    acc = None
    for plane, other in zip(planes, others):
        term = plane * other
        acc = term if acc is None else acc + term
    blocks = acc.shape[0]
    folded = acc[0:8]
    for g in range(1, blocks // 8):
        folded = folded + acc[8 * g : 8 * g + 8]
    products_ref[pl.ds(pl.multiple_of(8 * s, 8), 8)] = folded


def inner_products(newest, past_ref, products_ref):
    past = past_ref.shape[1]

    def several(i, carry):
        for k in range(3):
            s = 3 * i + k
            plane_products(newest, [past_ref[c, s].astype(F32) for c in range(3)], products_ref, s)
        return carry

    lax.fori_loop(0, past // 3, several, 0)


def product_row(products_ref):
    snaps = products_ref.shape[0] // 8
    sums = products_ref[pl.ds(0, snaps, stride=8)]
    for q in range(1, 8):
        sums = sums + products_ref[pl.ds(q, snaps, stride=8)]
    return lax.dot_general(jnp.ones((8, sums.shape[1]), F32), sums, NT, precision=HI)


def flow_kernel(
    codes_ref, state_ref, flags_ref, gram_ref, start_ref, past_hbm,
    out_ref, speed_1, speed_2, rows_out, gram_out, basis_ref,
    ext_1, ext_2, middle, past, products, rows, piece, near_slots, long_slots, row_slots,
    past_sem, send_1, recv_1, send_2, recv_2, near_send, near_recv, long_send, long_recv,
    all_send, all_recv, row_send, row_recv,
):
    near, z, y = groups()
    blocks, part = flags_ref.shape
    snaps = gram_ref.shape[0]
    size = snaps // LONG
    load = pltpu.make_async_copy(past_hbm, past, past_sem)
    load.start()
    barrier = pltpu.get_barrier_semaphore()
    count = halo_greet(barrier)
    for group in (near, z, y):
        count = count + group_greet(barrier, *group)
    density = 1.0 + SEDIMENT_EXTRA * flags_ref[...].astype(F32)
    mass = density * VOLUME
    pressure = pressure_of(state_ref[pl.ds(6, blocks, stride=7)], density)
    for b in range(blocks):
        ext_1[1, b + 1, 0:6] = state_ref[7 * b : 7 * b + 6]
        ext_1[1, b + 1, 6:7] = mass[b : b + 1]
        ext_1[1, b + 1, 7:8] = pressure[b : b + 1]
    halo_clear(ext_1)
    halo_clear(ext_2)
    products[pl.ds(8 * (snaps - 2), 16)] = jnp.zeros((16, part), F32)
    pl.semaphore_wait(barrier, count)

    halo_start(ext_1, send_1, recv_1)
    scatter = group_copies(
        *near, lambda other: gram_ref.at[shard_of(other, size)], lambda step: near_slots.at[step], near_send, near_recv
    )
    start(scatter)
    basis_ref[...] = start_ref[...]

    @pl.loop(0, 2)
    def _(i):
        basis_ref[...] = orthonormal_rows(basis_ref[...])

    halo_finish(ext_1, send_1, recv_1)
    forces(codes_ref, ext_1, state_ref, middle, speed_1, ext_2)

    finish(scatter)
    piece[0] = total(gram_ref[shard_of(near[0], size)], near_slots)
    over_z = group_copies(*z, lambda other: piece.at[0], lambda step: long_slots.at[0, step], long_send.at[0], long_recv.at[0])
    halo_start(ext_2, send_2, recv_2)
    start(over_z)
    load.wait()
    first = rounded(speed_1)
    inner_products(first, past, products)
    plane_products(first, first, products, snaps - 2)
    rows[0] = product_row(products)
    finish(over_z)
    piece[1] = total(piece[0], long_slots.at[0])
    over_y = group_copies(*y, lambda other: piece.at[1], lambda step: long_slots.at[1, step], long_send.at[1], long_recv.at[1])
    start(over_y)
    halo_finish(ext_2, send_2, recv_2)
    forces(codes_ref, ext_2, middle, out_ref, speed_2)

    finish(over_y)
    whole = total(piece[1], long_slots.at[1])
    piece[2] = whole
    gram_out[shard_of(near[0], size)] = whole
    second = rounded(speed_2)
    inner_products(second, past, products)
    plane_products(second, rounded(speed_1), products, snaps - 2)
    plane_products(second, second, products, snaps - 1)
    eight = lax.broadcasted_iota(jnp.int32, (8, snaps), 0)
    value = jnp.where(eight == 0, rows[0], product_row(products))
    gathers = group_copies(*near, lambda other: piece.at[2], lambda step: gram_out.at[shard_of(near[0], size)], all_send, all_recv)
    for stage, group in enumerate((z, y, near)):
        rows[1 + stage] = value
        copies = group_copies(
            *group, lambda other: rows.at[1 + stage], lambda step: row_slots.at[stage, step],
            row_send.at[stage], row_recv.at[stage],
        )
        start(copies)
        if stage == 0:
            start(gathers)
        finish(copies)
        value = total(value, row_slots.at[stage])
    rows_out[...] = value
    finish(gathers)


def flow(codes, state, flags, gram, start_rows, past):
    blocks, part = flags.shape
    rank, snaps = start_rows.shape
    shard = snaps // LONG
    dma = pltpu.SemaphoreType.DMA
    ext = pltpu.VMEM((3, blocks + 2, 8, part), F32)
    shapes = [state.shape, (3, blocks, part), (3, blocks, part), (8, snaps), (snaps, snaps), (rank, snaps)]
    return pl.pallas_call(
        flow_kernel,
        out_shape=[jax.ShapeDtypeStruct(shape, F32) for shape in shapes],
        in_specs=[pl.BlockSpec(memory_space=pltpu.SMEM), VM, VM, VM, VM, pl.BlockSpec(memory_space=pl.ANY)],
        out_specs=[VM] * len(shapes),
        scratch_shapes=[
            ext, ext,
            pltpu.VMEM(state.shape, F32),
            pltpu.VMEM(past.shape, BF),
            pltpu.VMEM((8 * snaps, part), F32),
            pltpu.VMEM((4, 8, snaps), F32),
            pltpu.VMEM((3, shard, snaps), F32),
            pltpu.VMEM((LONG, shard, snaps), F32),
            pltpu.VMEM((2, LONG, shard, snaps), F32),
            pltpu.VMEM((3, LONG, 8, snaps), F32),
            dma, dma((8,)), dma((8,)), dma((8,)), dma((8,)), dma((LONG,)), dma((LONG,)), dma((2, LONG)), dma((2, LONG)),
            dma((LONG,)), dma((LONG,)), dma((3, LONG)), dma((3, LONG)),
        ],
        compiler_params=pltpu.CompilerParams(collective_id=0, has_side_effects=True),
        name="flow",
    )(codes, state, flags, gram, start_rows, past)


def modes_kernel(gram_ref, rows_ref, basis_ref, speed_1, speed_2, past_hbm, out_ref, full_ref, past, weights, past_sem):
    width = gram_ref.shape[0]
    load = pltpu.make_async_copy(past_hbm, past, past_sem)
    load.start()
    rows = rows_ref[...]
    across = jnp.transpose(jnp.concatenate([rows, jnp.zeros((width - rows.shape[0], width), F32)], axis=0))
    lane = lax.broadcasted_iota(jnp.int32, (width, width), 1)
    row = lax.broadcasted_iota(jnp.int32, (width, width), 0)
    full = gram_ref[...]
    for k in range(2):
        place = width - 2 + k
        full = jnp.where(lane == place, jnp.broadcast_to(across[:, k : k + 1], full.shape), full)
        full = jnp.where(row == place, jnp.broadcast_to(rows[k : k + 1], full.shape), full)
    full_ref[...] = full

    def times_gram(t):
        return lax.dot_general(t, full_ref[...], NN, precision=HI)

    def half(i, t):
        t = orthonormal_rows(t)
        again = jnp.logical_and(i % 2 == 1, i < 2 * POD_ITERS - 1)
        return lax.cond(again, times_gram, lambda t: t, t)

    t = lax.fori_loop(0, 2 * POD_ITERS, half, times_gram(basis_ref[...]))
    last = jnp.broadcast_to(t[:, width - 1 : width], t.shape)
    weights[...] = lax.dot_general(t, last, TN, precision=HI)
    load.wait()
    snaps = past.shape[1]

    def several(i, sums):
        for k in range(3):
            s = 3 * i + k
            weight = jnp.broadcast_to(weights[pl.ds(s, 1)], sums[0].shape)
            sums = tuple(total + past[c, s].astype(F32) * weight for c, total in enumerate(sums))
        return sums

    zero = jnp.zeros(speed_1.shape[1:], F32)
    sums = lax.fori_loop(0, snaps // 3, several, (zero, zero, zero))
    for k, speed_ref in enumerate((speed_1, speed_2)):
        weight = jnp.broadcast_to(weights[width - 2 + k : width - 1 + k], zero.shape)
        sums = [total + plane * weight for total, plane in zip(sums, rounded(speed_ref))]
    for c in range(3):
        out_ref[pl.ds(c, zero.shape[0], stride=3)] = sums[c]


def modes(gram, rows, basis, speed_1, speed_2, past):
    components, _, blocks, part = past.shape
    return pl.pallas_call(
        modes_kernel,
        out_shape=jax.ShapeDtypeStruct((components * blocks, part), F32),
        in_specs=[VM] * 5 + [pl.BlockSpec(memory_space=pl.ANY)],
        out_specs=VM,
        scratch_shapes=[
            pltpu.VMEM(gram.shape, F32),
            pltpu.VMEM(past.shape, BF),
            pltpu.VMEM(gram.shape, F32),
            pltpu.SemaphoreType.DMA,
        ],
        name="modes",
    )(gram, rows, basis, speed_1, speed_2, past)


def body(particles, phase_flags, neighbours, history, basis_start):
    blocks, _, fields, part = particles.shape
    state = particles.reshape(blocks * fields, part)
    past = jnp.transpose(history[:, 0], (1, 2, 0, 3))
    gram = jnp.einsum("csbp,ctbp->st", past, past, preferred_element_type=F32)
    gram = jnp.pad(gram, ((0, 2), (0, 2)))
    state, speed_1, speed_2, rows, gram, basis = flow(
        neighbours[:, 0].T, state, phase_flags[:, 0], gram, basis_start.T, past
    )
    filtered = modes(gram, rows, basis, speed_1, speed_2, past)
    return (state.reshape(particles.shape), filtered.reshape(blocks, 1, 3, part))


def solution(mesh):
    in_specs = (
        P("stream", "vert", None, None),
        P("stream", "vert", None),
        P("stream", "vert", None),
        P("stream", "vert", None, None, None),
        P(),
    )
    out_specs = (P("stream", "vert", None, None), P("stream", "vert", None, None))
    return jax.shard_map(body, mesh=mesh, in_specs=in_specs, out_specs=out_specs, check_vma=False)
```

time: 114 us -> 86.8 us (0.76)
  Pallas kernels: 97.4 us -> 78.6 us
  other arithmetic: 3.44 us -> 0 us
  matrix products: 8.34 us -> 6.11 us
  local copies, waits for them, and re-layouts: 3.43 us -> 1.3 us
    pallas_call x7 -> x2, Pallas kernels: 97.4 us -> 78.6 us  [the longest x1 58 us: flow(): pl.pallas_call(flow_kernel, out_shape=[jax.ShapeDtypeStruct(shape, F32) f...]
    dot_general x2 -> x0, matrix products: 2.08 us -> none  [the longest x1 1.84 us: body(): jnp.einsum('kcbp,csbp->ks', newest, past, preferred_element_type=F32)]
    slice x1 -> x0, local copies, waits for them, and re-layouts: 1.43 us -> none  [body(): filtered = filtered + weights[snaps - 2 + k] * newest[k].astype(F32)]
    broadcast_in_dim x1 -> x0, other arithmetic: 1.26 us -> none  [body(): return (state.reshape(particles.shape), filtered[:, None])]
where the time goes in v4:
time: 86.8 us; the launch traced here: 86.7 us
  Pallas kernels  78.6 us (91%)
  matrix products  6.11 us (7%)
  local copies, waits for them, and re-layouts  1.3 us (1%)
    pallas_call x1, Pallas kernels, flow(): pl.pallas_call(flow_kernel, out_shape=[jax.ShapeDtypeStruct(shape, F32) f...  58 us
    pallas_call x1, Pallas kernels, modes(): pl.pallas_call(modes_kernel, out_shape=jax.ShapeDtypeStruct((components *...  20.6 us
    dot_general x1, matrix products, body(): gram = jnp.einsum('csbp,ctbp->st', past, past, preferred_element_type=F32)  6.11 us

profile of v4, /device:TPU:1, one launch (start us, length us, event | category | flops | bytes accessed | tf_op | source)
XLA Modules:
  0.0 86.7 jit_solution(12698996450935206239)
XLA Ops:
  0.6 6.1 %fusion.2 = f32[126,126]{1,0:T(8,128)S(1)} fusion(bf16[3,126,32,128]{3,2,1,0:T(8,128)(2,1)} %bitcast.15), kind=kOutput, calls=%fused_computation.2 | convolution fusion | flops 390168576 | bytes 3160080 | tf_op jit(solution)/shard_map/csbp,ctbp->st/dot_general | solution.py:496
  6.7 0.6 pad.4.gram_ref
  7.4 58.0 %flow.1 = (f32[224,128]{1,0:T(8,128)}, f32[3,32,128]{2,1,0:T(8,128)}, f32[3,32,128]{2,1,0:T(8,128)}, f32[8,128]{1,0:T(8,128)}, f32[128,128]{1,0:T(8,128)}, /*index=5*/f32[64,128]{1,0:T(8,128)}) custom-call(s32[4,32]{1,0:T(4,128)} %bitcast.23, f32[224,128]{1,0:T(8,128)} %bitcast.19, s32[32,128]{1,0:T(8,128)} %bitcast.22, f32[128,128]{1,0:T(8,128)} %pad.4.gram_ref, ...), custom_call_target="tpu_custom_call" | custom-call | tf_op jit(solution)/shard_map/flow/pallas_call | solution.py:407
  65.4 0.0 copy-start
  65.4 20.6 %modes.1 = f32[96,128]{1,0:T(8,128)} custom-call(f32[128,128]{1,0:T(8,128)} %get-tuple-element.9.gram_ref, f32[8,128]{1,0:T(8,128)} %get-tuple-element.10.rows_ref, f32[64,128]{1,0:T(8,128)} %get-tuple-element.11.basis_ref, f32[3,32,128]{2,1,0:T(8,128)} %get-tuple-element.12.speed_1, f32[3,32,128]{2,1,0:T(8,128)} %get-tuple-element.13.speed_2, ...), custom_call_target="tpu_custom_call" | custom-call | tf_op jit(solution)/shard_map/modes/pallas_call | solution.py:477
  86.0 0.0 copy-done
  86.0 0.6 copy.21
Async XLA Ops:
  65.4 20.6 %copy-start = (f32[224,128]{1,0:T(8,128)S(1)}, f32[224,128]{1,0:T(8,128)}, u32[]{:S(2)}) copy-start(f32[224,128]{1,0:T(8,128)} %get-tuple-element.8) | copy-start | bytes 344068

commit v5 on v4

--- a/solution.py
+++ b/solution.py
@@ -150,6 +150,7 @@
     return lax.dot_general(done, jnp.concatenate([zero, t], axis=0), NN, precision=HI)
 SIDES = [(ds, dv) for dv in (-1, 0, 1) for ds in (-1, 0, 1) if (ds, dv) != (0, 0)]
 LONG = 8
+JOIN = 8
 
 
 def present(ds, dv):
@@ -311,10 +312,63 @@
     return lax.dot_general(jnp.ones((8, sums.shape[1]), F32), sums, NT, precision=HI)
 
 
+def past_gram(past_ref, gram_ref):
+    past, blocks = past_ref.shape[1], past_ref.shape[2]
+    gram_ref[...] = jnp.zeros(gram_ref.shape, F32)
+    sums = jnp.zeros((past, past), F32)
+    for c in range(past_ref.shape[0]):
+        planes = jnp.swapaxes(past_ref[c], 0, 1)
+        for b in range(0, blocks, JOIN):
+            joined = jnp.concatenate([planes[b + k] for k in range(JOIN)], axis=1)
+            sums = sums + lax.dot_general(joined, joined, NT, preferred_element_type=F32)
+    gram_ref[0:past, 0:past] = sums
+
+
+def modes(gram_ref, rows, basis_ref, speed_1, speed_2, past, out_ref, full_ref, weights):
+    width = gram_ref.shape[0]
+    across = jnp.transpose(jnp.concatenate([rows, jnp.zeros((width - rows.shape[0], width), F32)], axis=0))
+    lane = lax.broadcasted_iota(jnp.int32, (width, width), 1)
+    row = lax.broadcasted_iota(jnp.int32, (width, width), 0)
+    full = gram_ref[...]
+    for k in range(2):
+        place = width - 2 + k
+        full = jnp.where(lane == place, jnp.broadcast_to(across[:, k : k + 1], full.shape), full)
+        full = jnp.where(row == place, jnp.broadcast_to(rows[k : k + 1], full.shape), full)
+    full_ref[...] = full
+
+    def times_gram(t):
+        return lax.dot_general(t, full_ref[...], NN, precision=HI)
+
+    def half(i, t):
+        t = orthonormal_rows(t)
+        again = jnp.logical_and(i % 2 == 1, i < 2 * POD_ITERS - 1)
+        return lax.cond(again, times_gram, lambda t: t, t)
+
+    t = lax.fori_loop(0, 2 * POD_ITERS, half, times_gram(basis_ref[...]))
+    last = jnp.broadcast_to(t[:, width - 1 : width], t.shape)
+    weights[...] = lax.dot_general(t, last, TN, precision=HI)
+    snaps = past.shape[1]
+
+    def several(i, sums):
+        for k in range(3):
+            s = 3 * i + k
+            weight = jnp.broadcast_to(weights[pl.ds(s, 1)], sums[0].shape)
+            sums = tuple(total + past[c, s].astype(F32) * weight for c, total in enumerate(sums))
+        return sums
+
+    zero = jnp.zeros(speed_1.shape[1:], F32)
+    sums = lax.fori_loop(0, snaps // 3, several, (zero, zero, zero))
+    for k, speed_ref in enumerate((speed_1, speed_2)):
+        weight = jnp.broadcast_to(weights[width - 2 + k : width - 1 + k], zero.shape)
+        sums = [total + plane * weight for total, plane in zip(sums, rounded(speed_ref))]
+    for c in range(3):
+        out_ref[pl.ds(c, zero.shape[0], stride=3)] = sums[c]
+
+
 def flow_kernel(
-    codes_ref, state_ref, flags_ref, gram_ref, start_ref, past_hbm,
-    out_ref, speed_1, speed_2, rows_out, gram_out, basis_ref,
-    ext_1, ext_2, middle, past, products, rows, piece, near_slots, long_slots, row_slots,
+    codes_ref, state_ref, flags_ref, start_ref, past_hbm,
+    out_ref, filtered_ref, speed_1, speed_2, gram_out, basis_ref, full, weights,
+    gram_ref, ext_1, ext_2, middle, past, products, rows, piece, near_slots, long_slots, row_slots,
     past_sem, send_1, recv_1, send_2, recv_2, near_send, near_recv, long_send, long_recv,
     all_send, all_recv, row_send, row_recv,
 ):
@@ -338,6 +392,8 @@
     halo_clear(ext_1)
     halo_clear(ext_2)
     products[pl.ds(8 * (snaps - 2), 16)] = jnp.zeros((16, part), F32)
+    load.wait()
+    past_gram(past, gram_ref)
     pl.semaphore_wait(barrier, count)
 
     halo_start(ext_1, send_1, recv_1)
@@ -359,7 +415,6 @@
     over_z = group_copies(*z, lambda other: piece.at[0], lambda step: long_slots.at[0, step], long_send.at[0], long_recv.at[0])
     halo_start(ext_2, send_2, recv_2)
     start(over_z)
-    load.wait()
     first = rounded(speed_1)
     inner_products(first, past, products)
     plane_products(first, first, products, snaps - 2)
@@ -393,28 +448,31 @@
             start(gathers)
         finish(copies)
         value = total(value, row_slots.at[stage])
-    rows_out[...] = value
+    rows[4] = value
     finish(gathers)
-
-
-def flow(codes, state, flags, gram, start_rows, past):
+    modes(gram_out, rows[4], basis_ref, speed_1, speed_2, past, filtered_ref, full, weights)
+
+
+def flow(codes, state, flags, start_rows, past):
     blocks, part = flags.shape
     rank, snaps = start_rows.shape
     shard = snaps // LONG
     dma = pltpu.SemaphoreType.DMA
     ext = pltpu.VMEM((3, blocks + 2, 8, part), F32)
-    shapes = [state.shape, (3, blocks, part), (3, blocks, part), (8, snaps), (snaps, snaps), (rank, snaps)]
+    shapes = [state.shape, (3 * blocks, part)]
+    square, speed = pltpu.VMEM((snaps, snaps), F32), pltpu.VMEM((3, blocks, part), F32)
     return pl.pallas_call(
         flow_kernel,
         out_shape=[jax.ShapeDtypeStruct(shape, F32) for shape in shapes],
-        in_specs=[pl.BlockSpec(memory_space=pltpu.SMEM), VM, VM, VM, VM, pl.BlockSpec(memory_space=pl.ANY)],
+        in_specs=[pl.BlockSpec(memory_space=pltpu.SMEM), VM, VM, VM, pl.BlockSpec(memory_space=pl.ANY)],
         out_specs=[VM] * len(shapes),
         scratch_shapes=[
+            speed, speed, square, pltpu.VMEM((rank, snaps), F32), square, square, square,
             ext, ext,
             pltpu.VMEM(state.shape, F32),
             pltpu.VMEM(past.shape, BF),
             pltpu.VMEM((8 * snaps, part), F32),
-            pltpu.VMEM((4, 8, snaps), F32),
+            pltpu.VMEM((5, 8, snaps), F32),
             pltpu.VMEM((3, shard, snaps), F32),
             pltpu.VMEM((LONG, shard, snaps), F32),
             pltpu.VMEM((2, LONG, shard, snaps), F32),
@@ -424,81 +482,16 @@
         ],
         compiler_params=pltpu.CompilerParams(collective_id=0, has_side_effects=True),
         name="flow",
-    )(codes, state, flags, gram, start_rows, past)
-
-
-def modes_kernel(gram_ref, rows_ref, basis_ref, speed_1, speed_2, past_hbm, out_ref, full_ref, past, weights, past_sem):
-    width = gram_ref.shape[0]
-    load = pltpu.make_async_copy(past_hbm, past, past_sem)
-    load.start()
-    rows = rows_ref[...]
-    across = jnp.transpose(jnp.concatenate([rows, jnp.zeros((width - rows.shape[0], width), F32)], axis=0))
-    lane = lax.broadcasted_iota(jnp.int32, (width, width), 1)
-    row = lax.broadcasted_iota(jnp.int32, (width, width), 0)
-    full = gram_ref[...]
-    for k in range(2):
-        place = width - 2 + k
-        full = jnp.where(lane == place, jnp.broadcast_to(across[:, k : k + 1], full.shape), full)
-        full = jnp.where(row == place, jnp.broadcast_to(rows[k : k + 1], full.shape), full)
-    full_ref[...] = full
-
-    def times_gram(t):
-        return lax.dot_general(t, full_ref[...], NN, precision=HI)
-
-    def half(i, t):
-        t = orthonormal_rows(t)
-        again = jnp.logical_and(i % 2 == 1, i < 2 * POD_ITERS - 1)
-        return lax.cond(again, times_gram, lambda t: t, t)
-
-    t = lax.fori_loop(0, 2 * POD_ITERS, half, times_gram(basis_ref[...]))
-    last = jnp.broadcast_to(t[:, width - 1 : width], t.shape)
-    weights[...] = lax.dot_general(t, last, TN, precision=HI)
-    load.wait()
-    snaps = past.shape[1]
-
-    def several(i, sums):
-        for k in range(3):
-            s = 3 * i + k
-            weight = jnp.broadcast_to(weights[pl.ds(s, 1)], sums[0].shape)
-            sums = tuple(total + past[c, s].astype(F32) * weight for c, total in enumerate(sums))
-        return sums
-
-    zero = jnp.zeros(speed_1.shape[1:], F32)
-    sums = lax.fori_loop(0, snaps // 3, several, (zero, zero, zero))
-    for k, speed_ref in enumerate((speed_1, speed_2)):
-        weight = jnp.broadcast_to(weights[width - 2 + k : width - 1 + k], zero.shape)
-        sums = [total + plane * weight for total, plane in zip(sums, rounded(speed_ref))]
-    for c in range(3):
-        out_ref[pl.ds(c, zero.shape[0], stride=3)] = sums[c]
-
-
-def modes(gram, rows, basis, speed_1, speed_2, past):
-    components, _, blocks, part = past.shape
-    return pl.pallas_call(
-        modes_kernel,
-        out_shape=jax.ShapeDtypeStruct((components * blocks, part), F32),
-        in_specs=[VM] * 5 + [pl.BlockSpec(memory_space=pl.ANY)],
-        out_specs=VM,
-        scratch_shapes=[
-            pltpu.VMEM(gram.shape, F32),
-            pltpu.VMEM(past.shape, BF),
-            pltpu.VMEM(gram.shape, F32),
-            pltpu.SemaphoreType.DMA,
-        ],
-        name="modes",
-    )(gram, rows, basis, speed_1, speed_2, past)
+    )(codes, state, flags, start_rows, past)
 
 
 def body(particles, phase_flags, neighbours, history, basis_start):
     blocks, _, fields, part = particles.shape
     state = particles.reshape(blocks * fields, part)
     past = jnp.transpose(history[:, 0], (1, 2, 0, 3))
-    gram = jnp.einsum("csbp,ctbp->st", past, past, preferred_element_type=F32)
-    gram = jnp.pad(gram, ((0, 2), (0, 2)))
-    state, speed_1, speed_2, rows, gram, basis = flow(
-        neighbours[:, 0].T, state, phase_flags[:, 0], gram, basis_start.T, past
+    state, filtered = flow(
+        neighbours[:, 0].T, state, phase_flags[:, 0], basis_start.T, past
     )
-    filtered = modes(gram, rows, basis, speed_1, speed_2, past)
     return (state.reshape(particles.shape), filtered.reshape(blocks, 1, 3, part))
 
 

time: 86.8 us -> 81.2 us (0.935)
  matrix products: 6.11 us -> 0 us
  local copies, waits for them, and re-layouts: 1.3 us -> 3.02 us
  Pallas kernels: 78.6 us -> 77.3 us
    pallas_call x1 -> x0, Pallas kernels: 20.6 us -> none  [modes(): pl.pallas_call(modes_kernel, out_shape=jax.ShapeDtypeStruct((components *...]
    pallas_call x1, Pallas kernels: 58 us -> 77.3 us  [flow(): pl.pallas_call(flow_kernel, out_shape=[jax.ShapeDtypeStruct(shape, F32) f...]
    dot_general x1 -> x0, matrix products: 6.11 us -> none  [body(): gram = jnp.einsum('csbp,ctbp->st', past, past, preferred_element_type=F32)]
    unnamed x3 -> x2, local copies, waits for them, and re-layouts: 0.65 us -> 3.02 us
where the time goes in v5:
time: 81.2 us; the launch traced here: 80.9 us
  Pallas kernels  77.3 us (95%)
  local copies, waits for them, and re-layouts  3.02 us (4%)
    pallas_call x1, Pallas kernels, flow(): pl.pallas_call(flow_kernel, out_shape=[jax.ShapeDtypeStruct(shape, F32) f...  77.3 us
    unnamed x2, local copies, waits for them, and re-layouts  3.02 us

profile of v5, /device:TPU:1, one launch (start us, length us, event | category | flops | bytes accessed | tf_op | source)
XLA Modules:
  0.0 80.9 jit_solution(14409899742367872207)
XLA Ops:
  0.6 77.3 %flow.1 = (f32[224,128]{1,0:T(8,128)}, f32[96,128]{1,0:T(8,128)}) custom-call(s32[4,32]{1,0:T(4,128)} %bitcast.17, f32[224,128]{1,0:T(8,128)} %bitcast.13, s32[32,128]{1,0:T(8,128)} %bitcast.16, f32[64,128]{1,0:T(8,128)} %bitcast.15, bf16[3,126,32,128]{3,2,1,0:T(8,128)(2,1)} %bitcast.11), custom_call_target="tpu_custom_call" | custom-call | tf_op jit(solution)/shard_map/flow/pallas_call | solution.py:464
  77.9 1.6 %copy.13 = f32[32,1,7,128]{3,1,2,0:T(1,128)} copy(f32[32,1,7,128]{3,1,2,0:T(1,128)} %bitcast.12) | data formatting | bytes 229376
  79.5 1.4 %copy.14 = f32[32,1,3,128]{3,1,2,0:T(1,128)} copy(f32[32,1,3,128]{3,1,2,0:T(1,128)} %bitcast.14) | data formatting | bytes 98304

commit v6 on v5

--- a/solution.py
+++ b/solution.py
@@ -39,7 +39,7 @@
     return a, b, x - a - b
 
 
-def forces(codes_ref, ext_ref, state_ref, out_ref, speed_ref, next_ref=None):
+def forces(codes_ref, ext_ref, state_ref, out_ref, speed_ref, next_ref=None, after_trip=None):
     blocks, part = ext_ref.shape[1] - 2, ext_ref.shape[3]
     row = lax.broadcasted_iota(jnp.int32, (8, part), 0)
 
@@ -116,6 +116,8 @@
     def several(i, carry):
         for k in range(TRIP):
             one_block(TRIP * i + k)
+        if after_trip is not None:
+            after_trip(i)
         return carry
 
     lax.fori_loop(0, blocks // TRIP, several, 0)
@@ -205,22 +207,58 @@
                 ext_ref[1 + dv, 0 if ds < 0 else blocks + 1] = jnp.zeros((fields, part), F32)
 
 
-def halo_start(ext_ref, send_sem, recv_sem):
-    for index in (1, 6, 0, 2, 3, 4, 5, 7):
+FACES = (1, 6)
+ENDS = (0, 2, 3, 4, 5, 7)
+
+
+def halo_start(ext_ref, send_sem, recv_sem, indices):
+    for index in indices:
 
         @pl.when(present(*SIDES[index]))
         def _():
             halo_copy(ext_ref, send_sem, recv_sem, index).start()
 
 
-def halo_finish(ext_ref, send_sem, recv_sem):
-    for index, (ds, dv) in enumerate(SIDES):
+def halo_finish(ext_ref, send_sem, recv_sem, indices):
+    for index in indices:
+        ds, dv = SIDES[index]
         back = SIDES.index((-ds, -dv))
 
         @pl.when(present(ds, dv))
         def _():
             halo_copy(ext_ref, send_sem, recv_sem, index).wait_send()
             halo_copy(ext_ref, send_sem, recv_sem, back).wait_recv()
+
+
+def face_copy(ext_ref, send_sem, recv_sem, side, trip):
+    dv = SIDES[FACES[side]][1]
+    rows = pl.ds(1 + TRIP * trip, TRIP)
+    return pltpu.make_async_remote_copy(
+        src_ref=ext_ref.at[1, rows],
+        dst_ref=ext_ref.at[1 - dv, rows],
+        send_sem=send_sem.at[side, trip],
+        recv_sem=recv_sem.at[side, trip],
+        device_id=(lax.axis_index("stream"), lax.axis_index("vert") + dv),
+        device_id_type=MESH,
+    )
+
+
+def face_start(ext_ref, send_sem, recv_sem, trip):
+    for side in range(2):
+
+        @pl.when(present(*SIDES[FACES[side]]))
+        def _():
+            face_copy(ext_ref, send_sem, recv_sem, side, trip).start()
+
+
+def face_finish(ext_ref, send_sem, recv_sem, trips):
+    for side in range(2):
+
+        @pl.when(present(*SIDES[FACES[side]]))
+        def _():
+            for trip in range(trips):
+                face_copy(ext_ref, send_sem, recv_sem, side, trip).wait_send()
+                face_copy(ext_ref, send_sem, recv_sem, 1 - side, trip).wait_recv()
 
 
 def groups():
@@ -369,7 +407,7 @@
     codes_ref, state_ref, flags_ref, start_ref, past_hbm,
     out_ref, filtered_ref, speed_1, speed_2, gram_out, basis_ref, full, weights,
     gram_ref, ext_1, ext_2, middle, past, products, rows, piece, near_slots, long_slots, row_slots,
-    past_sem, send_1, recv_1, send_2, recv_2, near_send, near_recv, long_send, long_recv,
+    past_sem, face_send, face_recv, send_1, recv_1, send_2, recv_2, near_send, near_recv, long_send, long_recv,
     all_send, all_recv, row_send, row_recv,
 ):
     near, z, y = groups()
@@ -396,7 +434,7 @@
     past_gram(past, gram_ref)
     pl.semaphore_wait(barrier, count)
 
-    halo_start(ext_1, send_1, recv_1)
+    halo_start(ext_1, send_1, recv_1, FACES + ENDS)
     scatter = group_copies(
         *near, lambda other: gram_ref.at[shard_of(other, size)], lambda step: near_slots.at[step], near_send, near_recv
     )
@@ -407,23 +445,32 @@
     def _(i):
         basis_ref[...] = orthonormal_rows(basis_ref[...])
 
-    halo_finish(ext_1, send_1, recv_1)
-    forces(codes_ref, ext_1, state_ref, middle, speed_1, ext_2)
-
     finish(scatter)
     piece[0] = total(gram_ref[shard_of(near[0], size)], near_slots)
     over_z = group_copies(*z, lambda other: piece.at[0], lambda step: long_slots.at[0, step], long_send.at[0], long_recv.at[0])
-    halo_start(ext_2, send_2, recv_2)
     start(over_z)
+    halo_finish(ext_1, send_1, recv_1, FACES + ENDS)
+
+    def send_previous(i):
+        @pl.when(i > 0)
+        def _():
+            face_start(ext_2, face_send, face_recv, i - 1)
+
+    forces(codes_ref, ext_1, state_ref, middle, speed_1, ext_2, send_previous)
+
+    trips = blocks // TRIP
+    finish(over_z)
+    piece[1] = total(piece[0], long_slots.at[0])
+    face_start(ext_2, face_send, face_recv, trips - 1)
+    halo_start(ext_2, send_2, recv_2, ENDS)
+    over_y = group_copies(*y, lambda other: piece.at[1], lambda step: long_slots.at[1, step], long_send.at[1], long_recv.at[1])
+    start(over_y)
     first = rounded(speed_1)
     inner_products(first, past, products)
     plane_products(first, first, products, snaps - 2)
     rows[0] = product_row(products)
-    finish(over_z)
-    piece[1] = total(piece[0], long_slots.at[0])
-    over_y = group_copies(*y, lambda other: piece.at[1], lambda step: long_slots.at[1, step], long_send.at[1], long_recv.at[1])
-    start(over_y)
-    halo_finish(ext_2, send_2, recv_2)
+    halo_finish(ext_2, send_2, recv_2, ENDS)
+    face_finish(ext_2, face_send, face_recv, trips)
     forces(codes_ref, ext_2, middle, out_ref, speed_2)
 
     finish(over_y)
@@ -477,12 +524,27 @@
             pltpu.VMEM((LONG, shard, snaps), F32),
             pltpu.VMEM((2, LONG, shard, snaps), F32),
             pltpu.VMEM((3, LONG, 8, snaps), F32),
-            dma, dma((8,)), dma((8,)), dma((8,)), dma((8,)), dma((LONG,)), dma((LONG,)), dma((2, LONG)), dma((2, LONG)),
+            dma, dma((2, blocks // TRIP)), dma((2, blocks // TRIP)), dma((8,)), dma((8,)), dma((8,)), dma((8,)), dma((LONG,)), dma((LONG,)), dma((2, LONG)), dma((2, LONG)),
             dma((LONG,)), dma((LONG,)), dma((3, LONG)), dma((3, LONG)),
         ],
         compiler_params=pltpu.CompilerParams(collective_id=0, has_side_effects=True),
         name="flow",
     )(codes, state, flags, start_rows, past)
+
+
+def deliver_kernel(state_ref, filtered_ref, state_out, filtered_out):
+    state_out[...] = state_ref[...]
+    filtered_out[...] = filtered_ref[...]
+
+
+def deliver(*arrays):
+    return pl.pallas_call(
+        deliver_kernel,
+        out_shape=[jax.ShapeDtypeStruct(array.shape, F32) for array in arrays],
+        in_specs=[VM, VM],
+        out_specs=[VM, VM],
+        name="deliver",
+    )(*arrays)
 
 
 def body(particles, phase_flags, neighbours, history, basis_start):
@@ -492,6 +554,7 @@
     state, filtered = flow(
         neighbours[:, 0].T, state, phase_flags[:, 0], basis_start.T, past
     )
+    state, filtered = deliver(state, filtered)
     return (state.reshape(particles.shape), filtered.reshape(blocks, 1, 3, part))
 
 

time: 81.2 us -> 79.3 us (0.977)
  local copies, waits for them, and re-layouts: 3.02 us -> 0 us
  Pallas kernels: 77.3 us -> 78.5 us
    unnamed x2 -> x0, local copies, waits for them, and re-layouts: 3.02 us -> none
    pallas_call x0 -> x1, Pallas kernels: none -> 1.57 us  [deliver(): pl.pallas_call(deliver_kernel, out_shape=[jax.ShapeDtypeStruct(array.shap...]
where the time goes in v6:
time: 79.3 us; the launch traced here: 79.1 us
  Pallas kernels  78.5 us (99%)
    pallas_call x1, Pallas kernels, flow(): pl.pallas_call(flow_kernel, out_shape=[jax.ShapeDtypeStruct(shape, F32) f...  76.9 us

profile of v6, /device:TPU:1, one launch (start us, length us, event | category | flops | bytes accessed | tf_op | source)
XLA Modules:
  0.0 79.1 jit_solution(3382744602835825533)
XLA Ops:
  0.6 76.9 %flow.1 = (f32[224,128]{1,0:T(8,128)}, f32[96,128]{1,0:T(8,128)}) custom-call(s32[4,32]{1,0:T(4,128)} %bitcast.15, f32[224,128]{1,0:T(8,128)} %bitcast.12, s32[32,128]{1,0:T(8,128)} %bitcast.14, f32[64,128]{1,0:T(8,128)} %bitcast.13, bf16[3,126,32,128]{3,2,1,0:T(8,128)(2,1)} %bitcast.11), custom_call_target="tpu_custom_call" | custom-call | tf_op jit(solution)/shard_map/flow/pallas_call | solution.py:511
  77.6 1.6 %deliver.1 = (f32[224,128]{1,0:T(8,128)}, f32[96,128]{1,0:T(8,128)}) custom-call(f32[224,128]{1,0:T(8,128)} %get-tuple-element.6.state_ref, f32[96,128]{1,0:T(8,128)} %get-tuple-element.7.filtered_ref), custom_call_target="tpu_custom_call" | custom-call | tf_op jit(solution)/shard_map/deliver/pallas_call | solution.py:541

commit v7 on v6

--- a/solution.py
+++ b/solution.py
@@ -482,20 +482,23 @@
     plane_products(second, rounded(speed_1), products, snaps - 2)
     plane_products(second, second, products, snaps - 1)
     eight = lax.broadcasted_iota(jnp.int32, (8, snaps), 0)
-    value = jnp.where(eight == 0, rows[0], product_row(products))
+    value = jnp.where(eight == 0, rows[0], product_row(products))[0:2]
+    pair = pl.ds(0, 2)
     gathers = group_copies(*near, lambda other: piece.at[2], lambda step: gram_out.at[shard_of(near[0], size)], all_send, all_recv)
     for stage, group in enumerate((z, y, near)):
-        rows[1 + stage] = value
+        rows[1 + stage, 0:2] = value
         copies = group_copies(
-            *group, lambda other: rows.at[1 + stage], lambda step: row_slots.at[stage, step],
+            *group, lambda other: rows.at[1 + stage, pair], lambda step: row_slots.at[stage, step, pair],
             row_send.at[stage], row_recv.at[stage],
         )
         start(copies)
         if stage == 0:
             start(gathers)
         finish(copies)
-        value = total(value, row_slots.at[stage])
-    rows[4] = value
+        for step in range(1, LONG):
+            value = value + row_slots[stage, step, 0:2]
+    rows[4] = jnp.zeros(rows.shape[1:], F32)
+    rows[4, 0:2] = value
     finish(gathers)
     modes(gram_out, rows[4], basis_ref, speed_1, speed_2, past, filtered_ref, full, weights)
 

time: 79.3 us -> 78.9 us (level)
  no operation moved by 1% of the time
where the time goes in v7:
time: 78.9 us; the launch traced here: 78.7 us
  Pallas kernels  78 us (99%)
    pallas_call x1, Pallas kernels, flow(): pl.pallas_call(flow_kernel, out_shape=[jax.ShapeDtypeStruct(shape, F32) f...  76.4 us

profile of v7, /device:TPU:1, one launch (start us, length us, event | category | flops | bytes accessed | tf_op | source)
XLA Modules:
  0.0 78.7 jit_solution(1450787679030796447)
XLA Ops:
  0.6 76.4 %flow.1 = (f32[224,128]{1,0:T(8,128)}, f32[96,128]{1,0:T(8,128)}) custom-call(s32[4,32]{1,0:T(4,128)} %bitcast.15, f32[224,128]{1,0:T(8,128)} %bitcast.12, s32[32,128]{1,0:T(8,128)} %bitcast.14, f32[64,128]{1,0:T(8,128)} %bitcast.13, bf16[3,126,32,128]{3,2,1,0:T(8,128)(2,1)} %bitcast.11), custom_call_target="tpu_custom_call" | custom-call | tf_op jit(solution)/shard_map/flow/pallas_call | solution.py:514
  77.1 1.6 %deliver.1 = (f32[224,128]{1,0:T(8,128)}, f32[96,128]{1,0:T(8,128)}) custom-call(f32[224,128]{1,0:T(8,128)} %get-tuple-element.6.state_ref, f32[96,128]{1,0:T(8,128)} %get-tuple-element.7.filtered_ref), custom_call_target="tpu_custom_call" | custom-call | tf_op jit(solution)/shard_map/deliver/pallas_call | solution.py:544
